TPU v7x, 32 devices: a whole 2x2x4 slice. The times are simulated.
32 devices in a mesh: ctx: 16 (over z, x, core), fsdp: 2 (over y).
Axes of the slice: x: 2, y: 2, z: 4, core: 2. Of those that a mesh axis runs over, the one named last changes fastest.
Arguments:
- tokens: bfloat16 [2, 4096, 768], P('fsdp', 'ctx'), may hold values from -6 to 6
- query_weight: bfloat16 [768, 768], P('fsdp'), may hold values from -0.21875 to 0.21875
- query_bias: bfloat16 [768], P('fsdp'), may hold values from -1.5 to 1.5
- key_weight: bfloat16 [768, 768], P('fsdp'), may hold values from -0.21875 to 0.21875
- value_weight: bfloat16 [768, 768], P('fsdp'), may hold values from -0.21875 to 0.21875
- value_bias: bfloat16 [768], P('fsdp'), may hold values from -1.5 to 1.5
- out_weight: bfloat16 [768, 768], P('fsdp'), may hold values from -1.25 to 1.25
- out_bias: bfloat16 [768], P('fsdp'), may hold values from -1.5 to 1.5
- first_gain: bfloat16 [768], P('fsdp'), may hold values from 0.5 to 1.5
- first_shift: bfloat16 [768], P('fsdp'), may hold values from -1.5 to 1.5
- inner_weight: bfloat16 [768, 3072], P('fsdp'), may hold values from -0.21875 to 0.21875
- inner_bias: bfloat16 [3072], P('fsdp'), may hold values from -1.5 to 1.5
- outer_weight: bfloat16 [3072, 768], P('fsdp'), may hold values from -0.109375 to 0.109375
- outer_bias: bfloat16 [768], P('fsdp'), may hold values from -1.5 to 1.5
- second_gain: bfloat16 [768], P('fsdp'), may hold values from 0.5 to 1.5
- second_shift: bfloat16 [768], P('fsdp'), may hold values from -1.5 to 1.5
- doc_lengths: int32 [2, 48], P('fsdp'), may hold values from 1 to 2304, 4096 in all within a row
- grad_output: bfloat16 [2, 4096, 768], P('fsdp', 'ctx'), may hold values from -6 to 6
Outputs:
- output: bfloat16 [2, 4096, 768], P('fsdp', 'ctx')
- grad_tokens: float32 [2, 4096, 768], P('fsdp', 'ctx')
- grad_query_weight: float32 [768, 768], P('fsdp')
- grad_query_bias: float32 [768], P('fsdp')
- grad_key_weight: float32 [768, 768], P('fsdp')
- grad_value_weight: float32 [768, 768], P('fsdp')
- grad_value_bias: float32 [768], P('fsdp')
- grad_out_weight: float32 [768, 768], P('fsdp')
- grad_out_bias: float32 [768], P('fsdp')
- grad_first_gain: float32 [768], P('fsdp')
- grad_first_shift: float32 [768], P('fsdp')
- grad_inner_weight: float32 [768, 3072], P('fsdp')
- grad_inner_bias: float32 [3072], P('fsdp')
- grad_outer_weight: float32 [3072, 768], P('fsdp')
- grad_outer_bias: float32 [768], P('fsdp')
- grad_second_gain: float32 [768], P('fsdp')
- grad_second_shift: float32 [768], P('fsdp')
Inputs may be any that keep to these rules, and one draw needn't show every extreme that they name: `doc_lengths`: each row holds the 48 document lengths of one sequence in order; they sum to 4096 and the longest is exactly 2304.
All inputs are finite; a program needn't handle non-finite values.
Results may differ from a plain program's by a relative error of at most 0.018.
Values may be sent and summed in bfloat16 or wider, within the bound.
No kernel may reach another device: no remote copies, remote signals or barrier semaphores. Data moves between devices by JAX's collectives and lax.ppermute only.
A program may use at most 384 MiB of HBM per device.

v0:
```python
import math

import jax
import jax.numpy as jnp
from jax import lax
from jax.sharding import PartitionSpec as P

H = 12
HD = 64


eps = 1e-12


def layer_norm(r, gain, shift):
    mean = jnp.mean(r, axis=-1, keepdims=True)
    centered = r - mean
    var = jnp.mean(centered * centered, axis=-1, keepdims=True)
    return centered * lax.rsqrt(var + eps) * gain + shift


def gelu_exact(v):
    return jax.nn.gelu(v, approximate=False)


def inner_rows(left, right):
    return lax.dot_general(
        left, right, (((1,), (1,)), ((), ())), preferred_element_type=jnp.float32
    )


def inner_cols(left, right):
    return lax.dot_general(
        left, right, (((0,), (0,)), ((), ())), preferred_element_type=jnp.float32
    )


def segment_of(places, lengths):
    ends = jnp.cumsum(lengths)
    return jnp.sum((places[:, None] >= ends[None, :]).astype(jnp.int32), axis=1)


def masked_scores(query_part, key_part, allowed, scale):
    raw = inner_rows(query_part, key_part) * scale
    return jnp.where(allowed, raw, jnp.float32(-1e30))


def on_device(
    tokens,
    query_weight,
    query_bias,
    key_weight,
    value_weight,
    value_bias,
    out_weight,
    out_bias,
    first_gain,
    first_shift,
    inner_weight,
    inner_bias,
    outer_weight,
    outer_bias,
    second_gain,
    second_shift,
    doc_lengths,
    grad_output,
):
    rows = tokens.shape[1]
    width = tokens.shape[2]
    scale = 1.0 / math.sqrt(HD)
    length_total = rows * lax.axis_size("ctx")
    gathered = (
        lax.all_gather(query_weight, "fsdp", axis=0, tiled=True),
        lax.all_gather(query_bias, "fsdp", axis=0, tiled=True),
        lax.all_gather(key_weight, "fsdp", axis=0, tiled=True),
        lax.all_gather(value_weight, "fsdp", axis=0, tiled=True),
        lax.all_gather(value_bias, "fsdp", axis=0, tiled=True),
        lax.all_gather(out_weight, "fsdp", axis=0, tiled=True),
        lax.all_gather(out_bias, "fsdp", axis=0, tiled=True),
        lax.all_gather(first_gain, "fsdp", axis=0, tiled=True),
        lax.all_gather(first_shift, "fsdp", axis=0, tiled=True),
        lax.all_gather(inner_weight, "fsdp", axis=0, tiled=True),
        lax.all_gather(inner_bias, "fsdp", axis=0, tiled=True),
        lax.all_gather(outer_weight, "fsdp", axis=0, tiled=True),
        lax.all_gather(outer_bias, "fsdp", axis=0, tiled=True),
        lax.all_gather(second_gain, "fsdp", axis=0, tiled=True),
        lax.all_gather(second_shift, "fsdp", axis=0, tiled=True),
    )
    (
        query_full,
        qbias_full,
        key_full,
        value_full,
        vbias_full,
        out_full,
        obias_full,
        gain_one,
        shift_one,
        inner_full,
        ibias_full,
        outer_full,
        outbias_full,
        gain_two,
        shift_two,
    ) = gathered
    local_in = tokens[0]
    local_float = local_in.astype(jnp.float32)
    query_low = (
        jnp.dot(local_in, query_full, preferred_element_type=jnp.float32)
        + qbias_full.astype(jnp.float32)
    ).astype(jnp.bfloat16)
    key_low = jnp.dot(local_in, key_full, preferred_element_type=jnp.float32).astype(jnp.bfloat16)
    value_low = (
        jnp.dot(local_in, value_full, preferred_element_type=jnp.float32)
        + vbias_full.astype(jnp.float32)
    ).astype(jnp.bfloat16)
    first_row = lax.axis_index("ctx") * rows
    places_own = first_row + jnp.arange(rows, dtype=jnp.int32)
    segs_own = segment_of(places_own, doc_lengths[0])
    keys_all, values_all = (
        lax.all_gather(key_low, "ctx", axis=0, tiled=True),
        lax.all_gather(value_low, "ctx", axis=0, tiled=True),
    )
    places_all = jnp.arange(length_total, dtype=jnp.int32)
    segs_all = segment_of(places_all, doc_lengths[0])
    allowed = segs_own[:, None] == segs_all[None, :]
    head_outs = []
    log_list = []
    for head in range(H):
        cols = slice(head * HD, (head + 1) * HD)
        scores = masked_scores(query_low[:, cols], keys_all[:, cols], allowed, scale)
        top = jnp.max(scores, axis=1, keepdims=True)
        expd = jnp.exp(scores - top)
        total = jnp.sum(expd, axis=1, keepdims=True)
        probs_low = (expd / total).astype(jnp.bfloat16)
        head_outs.append(
            jnp.dot(probs_low, values_all[:, cols], preferred_element_type=jnp.float32)
        )
        log_list.append(top[:, 0] + jnp.log(total[:, 0]))
    attn_low = jnp.concatenate(head_outs, axis=1).astype(jnp.bfloat16)
    log_sums = jnp.stack(log_list, axis=0)
    branch = jnp.dot(attn_low, out_full, preferred_element_type=jnp.float32) + obias_full.astype(
        jnp.float32
    )
    hidden, first_back = jax.vjp(
        layer_norm,
        local_float + branch,
        gain_one.astype(jnp.float32),
        shift_one.astype(jnp.float32),
    )
    hidden_low = hidden.astype(jnp.bfloat16)
    inner = jnp.dot(hidden_low, inner_full, preferred_element_type=jnp.float32) + ibias_full.astype(
        jnp.float32
    )
    active, gelu_back = jax.vjp(gelu_exact, inner)
    active_low = active.astype(jnp.bfloat16)
    outer = jnp.dot(
        active_low, outer_full, preferred_element_type=jnp.float32
    ) + outbias_full.astype(jnp.float32)
    result, second_back = jax.vjp(
        layer_norm, hidden + outer, gain_two.astype(jnp.float32), shift_two.astype(jnp.float32)
    )
    output = result.astype(jnp.bfloat16)[None]
    grad_y = grad_output[0].astype(jnp.float32)
    d_second, grad_gain_two, grad_shift_two = second_back(grad_y)
    d_outer_low = d_second.astype(jnp.bfloat16)
    grad_outbias = jnp.sum(d_outer_low.astype(jnp.float32), axis=0)
    grad_outer = inner_cols(active_low, d_outer_low)
    d_active = inner_rows(d_outer_low, outer_full)
    (d_inner,) = gelu_back(d_active)
    d_inner_low = d_inner.astype(jnp.bfloat16)
    grad_ibias = jnp.sum(d_inner_low.astype(jnp.float32), axis=0)
    grad_inner = inner_cols(hidden_low, d_inner_low)
    d_hidden = d_second + inner_rows(d_inner_low, inner_full)
    d_first, grad_gain_one, grad_shift_one = first_back(d_hidden)
    d_branch_low = d_first.astype(jnp.bfloat16)
    grad_obias = jnp.sum(d_branch_low.astype(jnp.float32), axis=0)
    grad_out = inner_cols(attn_low, d_branch_low)
    d_attn_low = inner_rows(d_branch_low, out_full).astype(jnp.bfloat16)
    dq_list = []
    dk_list = []
    dv_list = []
    for head in range(H):
        cols = slice(head * HD, (head + 1) * HD)
        scores = masked_scores(query_low[:, cols], keys_all[:, cols], allowed, scale)
        probs = jnp.exp(scores - log_sums[head][:, None])
        d_probs = inner_rows(d_attn_low[:, cols], values_all[:, cols])
        delta = jnp.sum(probs * d_probs, axis=1)
        d_scores = (probs * (d_probs - delta[:, None])).astype(jnp.bfloat16)
        dq_list.append(
            jnp.dot(d_scores, keys_all[:, cols], preferred_element_type=jnp.float32) * scale
        )
        dk_list.append(inner_cols(d_scores, query_low[:, cols]) * scale)
        dv_list.append(inner_cols(probs.astype(jnp.bfloat16), d_attn_low[:, cols]))
    key_terms = jnp.concatenate(dk_list + dv_list, axis=1)
    shares = lax.psum_scatter(
        key_terms.astype(jnp.bfloat16), "ctx", scatter_dimension=0, tiled=True
    ).astype(jnp.float32)
    d_key_low = shares[:, :width].astype(jnp.bfloat16)
    d_value_low = shares[:, width:].astype(jnp.bfloat16)
    d_query_low = jnp.concatenate(dq_list, axis=1).astype(jnp.bfloat16)
    grad_qbias = jnp.sum(d_query_low.astype(jnp.float32), axis=0)
    grad_vbias = jnp.sum(d_value_low.astype(jnp.float32), axis=0)
    grad_query = inner_cols(local_in, d_query_low)
    grad_key = inner_cols(local_in, d_key_low)
    grad_value = inner_cols(local_in, d_value_low)
    grad_input = (
        d_first
        + inner_rows(d_query_low, query_full)
        + inner_rows(d_key_low, key_full)
        + inner_rows(d_value_low, value_full)
    )
    shards = (
        lax.psum_scatter(
            grad_query.astype(jnp.bfloat16), "fsdp", scatter_dimension=0, tiled=True
        ).astype(jnp.float32),
        lax.psum_scatter(
            grad_qbias.astype(jnp.bfloat16), "fsdp", scatter_dimension=0, tiled=True
        ).astype(jnp.float32),
        lax.psum_scatter(
            grad_key.astype(jnp.bfloat16), "fsdp", scatter_dimension=0, tiled=True
        ).astype(jnp.float32),
        lax.psum_scatter(
            grad_value.astype(jnp.bfloat16), "fsdp", scatter_dimension=0, tiled=True
        ).astype(jnp.float32),
        lax.psum_scatter(
            grad_vbias.astype(jnp.bfloat16), "fsdp", scatter_dimension=0, tiled=True
        ).astype(jnp.float32),
        lax.psum_scatter(
            grad_out.astype(jnp.bfloat16), "fsdp", scatter_dimension=0, tiled=True
        ).astype(jnp.float32),
        lax.psum_scatter(
            grad_obias.astype(jnp.bfloat16), "fsdp", scatter_dimension=0, tiled=True
        ).astype(jnp.float32),
        lax.psum_scatter(
            grad_gain_one.astype(jnp.bfloat16), "fsdp", scatter_dimension=0, tiled=True
        ).astype(jnp.float32),
        lax.psum_scatter(
            grad_shift_one.astype(jnp.bfloat16), "fsdp", scatter_dimension=0, tiled=True
        ).astype(jnp.float32),
        lax.psum_scatter(
            grad_inner.astype(jnp.bfloat16), "fsdp", scatter_dimension=0, tiled=True
        ).astype(jnp.float32),
        lax.psum_scatter(
            grad_ibias.astype(jnp.bfloat16), "fsdp", scatter_dimension=0, tiled=True
        ).astype(jnp.float32),
        lax.psum_scatter(
            grad_outer.astype(jnp.bfloat16), "fsdp", scatter_dimension=0, tiled=True
        ).astype(jnp.float32),
        lax.psum_scatter(
            grad_outbias.astype(jnp.bfloat16), "fsdp", scatter_dimension=0, tiled=True
        ).astype(jnp.float32),
        lax.psum_scatter(
            grad_gain_two.astype(jnp.bfloat16), "fsdp", scatter_dimension=0, tiled=True
        ).astype(jnp.float32),
        lax.psum_scatter(
            grad_shift_two.astype(jnp.bfloat16), "fsdp", scatter_dimension=0, tiled=True
        ).astype(jnp.float32),
    )
    totals = lax.psum(tuple(shards), "ctx")
    return (output, grad_input[None]) + tuple(totals)


def solution(mesh):
    placed = (
        P("fsdp", "ctx", None),
        P("fsdp", None),
        P("fsdp"),
        P("fsdp", None),
        P("fsdp", None),
        P("fsdp"),
        P("fsdp", None),
        P("fsdp"),
        P("fsdp"),
        P("fsdp"),
        P("fsdp", None),
        P("fsdp"),
        P("fsdp", None),
        P("fsdp"),
        P("fsdp"),
        P("fsdp"),
        P("fsdp", None),
        P("fsdp", "ctx", None),
    )
    return jax.shard_map(
        on_device,
        mesh=mesh,
        in_specs=placed,
        out_specs=(
            P("fsdp", "ctx", None),
            P("fsdp", "ctx", None),
            P("fsdp", None),
            P("fsdp"),
            P("fsdp", None),
            P("fsdp", None),
            P("fsdp"),
            P("fsdp", None),
            P("fsdp"),
            P("fsdp"),
            P("fsdp"),
            P("fsdp", None),
            P("fsdp"),
            P("fsdp", None),
            P("fsdp"),
            P("fsdp"),
            P("fsdp"),
        ),
        check_vma=False,
    )
```

profile of v0, /device:TPU:1, one launch (start us, length us, event | category | flops | bytes accessed | tf_op | source)
XLA Modules:
  0.0 1196.4 jit_solution(10272641338332044763)
XLA Ops:
  9.5 25.0 %all-gather.20.cloned.1.call-done = bf16[768,768]{1,0:T(8,128)(2,1)} async-done(((bf16[384,768]{1,0:T(8,128)(2,1)}), bf16[768,768]{1,0:T(8,128)(2,1)}) %all-gather.20.cloned.1.call-update) | async-done | bytes 1179664 | tf_op jit(solution)/shard_map/all_gather | solution.py:75
  38.0 3.2 all-gather.1
  41.2 17.6 %all-gather.24.cloned.1.call-done = bf16[768,768]{1,0:T(8,128)(2,1)} async-done(((bf16[384,768]{1,0:T(8,128)(2,1)}), bf16[768,768]{1,0:T(8,128)(2,1)}) %all-gather.24.cloned.1.call-update) | async-done | bytes 1179664 | tf_op jit(solution)/shard_map/all_gather | solution.py:76
  63.6 3.2 all-gather.6
  66.9 3.2 all-gather.5
  70.1 3.5 all-gather.2
  73.7 3.5 all-gather
  77.8 3.5 all-gather.4
  81.4 3.2 all-gather.3
  84.6 3.2 all-gather.7
  87.9 3.4 all-gather.8
  93.1 55.3 %all-gather.22.cloned.1.call-done = bf16[4096,768]{1,0:T(8,128)(2,1)} async-done(((bf16[256,768]{1,0:T(8,128)(2,1)}), bf16[4096,768]{1,0:T(8,128)(2,1)}) %all-gather.22.cloned.1.call-update) | async-done | bytes 6291472 | tf_op jit(solution)/shard_map/all_gather | solution.py:121
  151.2 3.1 fusion.293
  155.0 2.9 fusion.294
  158.6 3.3 fusion.295
  162.6 2.9 fusion.296
  166.2 3.1 fusion.297
  170.1 2.9 fusion.298
  173.7 3.5 fusion.299
  178.0 3.0 fusion.300
  181.7 3.1 fusion.301
  185.6 2.9 fusion.302
  189.2 3.1 fusion.303
  195.0 16.5 %all-gather.26.cloned.1.call-done = bf16[4096,768]{1,0:T(8,128)(2,1)} async-done(((bf16[256,768]{1,0:T(8,128)(2,1)}), bf16[4096,768]{1,0:T(8,128)(2,1)}) %all-gather.26.cloned.1.call-update) | async-done | bytes 6291472 | tf_op jit(solution)/shard_map/all_gather | solution.py:122
  211.5 3.6 fusion.146
  243.4 54.8 %all-gather.30.cloned.1.call-done = bf16[768,3072]{1,0:T(8,128)(2,1)} async-done(((bf16[384,3072]{1,0:T(8,128)(2,1)}), bf16[768,3072]{1,0:T(8,128)(2,1)}) %all-gather.30.cloned.1.call-update) | async-done | bytes 4718608 | tf_op jit(solution)/shard_map/all_gather | solution.py:82
  298.3 11.7 multiply_convert_fusion.12
  310.0 52.5 %all-gather.32.cloned.1.call-done = bf16[3072,768]{1,0:T(8,128)(2,1)} async-done(((bf16[1536,768]{1,0:T(8,128)(2,1)}), bf16[3072,768]{1,0:T(8,128)(2,1)}) %all-gather.32.cloned.1.call-update) | async-done | bytes 4718608 | tf_op jit(solution)/shard_map/all_gather | solution.py:84
  362.5 4.0 fusion.305
  368.6 2.7 fusion.287
  389.7 3.2 multiply_reduce_fusion.8
  392.9 4.9 multiply_convert_fusion.8
  397.8 3.0 multiply_reduce_fusion.7
  400.7 4.9 multiply_convert_fusion.7
  405.6 4.4 multiply_reduce_fusion.6
  410.0 4.9 multiply_convert_fusion.6
  414.9 4.2 multiply_reduce_fusion.5
  419.1 4.8 multiply_convert_fusion.5
  423.9 5.6 multiply_reduce_fusion.4
  429.5 6.2 multiply_convert_fusion.4
  435.7 5.3 multiply_reduce_fusion.3
  441.0 6.0 multiply_convert_fusion.3
  446.9 5.6 multiply_reduce_fusion.2
  452.5 5.9 multiply_convert_fusion.2
  458.5 5.3 multiply_reduce_fusion.1
  463.8 6.0 multiply_convert_fusion.1
  469.8 5.6 multiply_reduce_fusion
  475.4 5.9 multiply_convert_fusion
  481.3 3.1 fusion.3
  484.4 3.1 fusion.5
  524.0 4.1 fusion.113
  530.5 2.9 fusion.117
  535.7 2.9 fusion.121
  549.5 5.2 convolution_convert_fusion.1
  556.7 3.6 convolution_convert_fusion
  560.4 94.0 %reduce-scatter.14.cloned.1.call-done = bf16[256,1536]{0,1:T(8,128)(2,1)} async-done(((bf16[4096,1536]{0,1:T(8,128)(2,1)}), bf16[256,1536]{0,1:T(8,128)(2,1)}) %reduce-scatter.14.cloned.1.call-update) | async-done | bytes 786448 | tf_op jit(solution)/shard_map/reduce_scatter | solution.py:196
  669.1 9.6 reduce-scatter.22.cloned.1.call-done
  680.1 22.8 %reduce-scatter.16.cloned.1.call-done = bf16[384,768]{1,0:T(8,128)(2,1)} async-done(((bf16[768,768]{1,0:T(8,128)(2,1)}), bf16[384,768]{1,0:T(8,128)(2,1)}) %reduce-scatter.16.cloned.1.call-update) | async-done | bytes 589840 | tf_op jit(solution)/shard_map/reduce_scatter | solution.py:229
  702.9 62.8 %reduce-scatter.18.cloned.1.call-done = bf16[384,3072]{1,0:T(8,128)(2,1)} async-done(((bf16[768,3072]{1,0:T(8,128)(2,1)}), bf16[384,3072]{1,0:T(8,128)(2,1)}) %reduce-scatter.18.cloned.1.call-update) | async-done | bytes 2359312 | tf_op jit(solution)/shard_map/reduce_scatter | solution.py:241
  765.6 63.0 %reduce-scatter.20.cloned.1.call-done = bf16[1536,768]{1,0:T(8,128)(2,1)} async-done(((bf16[3072,768]{1,0:T(8,128)(2,1)}), bf16[1536,768]{1,0:T(8,128)(2,1)}) %reduce-scatter.20.cloned.1.call-update) | async-done | bytes 2359312 | tf_op jit(solution)/shard_map/reduce_scatter | solution.py:247
  828.8 6.0 all-reduce.10
  841.6 11.7 reduce-scatter.24.cloned.1.call-done
  854.6 23.1 %reduce-scatter.26.cloned.1.call-done = bf16[384,768]{1,0:T(8,128)(2,1)} async-done(((bf16[768,768]{1,0:T(8,128)(2,1)}), bf16[384,768]{1,0:T(8,128)(2,1)}) %reduce-scatter.26.cloned.1.call-update) | async-done | bytes 589840
  879.1 303.9 %all-reduce.12 = (f32[384,768]{0,1:T(8,128)}, f32[384]{0:T(512)}, f32[384,768]{0,1:T(8,128)}, f32[384,768]{0,1:T(8,128)S(1)}, f32[384]{0:T(512)}, /*index=5*/f32...) all-reduce(bf16[384,768]{0,1:T(8,128)(2,1)S(1)} %copy.52, ...), channel_id=1, replica_groups=mesh['ctx'=16,'fsdp'=2] {'ctx'}, use_global_device_ids=true, to_apply=%region_49.50 | all-reduce | flops 3543552 | bytes 21270528 | tf_op jit(solution)/shard_map/psum | solution.py:260
  (387 shorter events, 159.0 us)
Async XLA Ops:
  7.2 27.3 %all-gather.20.cloned.1.call-start = ((), (), s32[]{:S(2)}) async-start(), calls=%async_computation.8 | async-start | bytes 1769472 | tf_op jit(solution)/shard_map/all_gather | solution.py:75
  7.9 50.9 %all-gather.24.cloned.1.call-start = ((), (), s32[]{:S(2)}) async-start(), calls=%async_computation.10 | async-start | bytes 1769472 | tf_op jit(solution)/shard_map/all_gather | solution.py:76
  8.7 82.6 %all-gather.18.cloned.1.call-start = ((), (), s32[]{:S(2)}) async-start(), calls=%async_computation.7 | async-start | bytes 1769472 | tf_op jit(solution)/shard_map/all_gather | solution.py:73
  9.4 138.9 %all-gather.22.cloned.1.call-start = ((), (), s32[]{:S(2)}) async-start(), calls=%async_computation.9 | async-start | bytes 6684672 | tf_op jit(solution)/shard_map/all_gather | solution.py:121
  37.1 26.5 %copy-start.82 = (bf16[384]{0:T(512)(128)(2,1)S(1)}, bf16[384]{0:T(512)(128)(2,1)}, u32[]{:S(2)}) copy-start(bf16[384]{0:T(512)(128)(2,1)} %param.31) | copy-start | bytes 2308
  37.1 29.7 %copy-start.81 = (bf16[1536]{0:T(1024)(128)(2,1)S(1)}, bf16[1536]{0:T(1024)(128)(2,1)}, u32[]{:S(2)}) copy-start(bf16[1536]{0:T(1024)(128)(2,1)} %param.29) | copy-start | bytes 9220
  37.1 33.0 %copy-start.83 = (bf16[384]{0:T(512)(128)(2,1)S(1)}, bf16[384]{0:T(512)(128)(2,1)}, u32[]{:S(2)}) copy-start(bf16[384]{0:T(512)(128)(2,1)} %param.25) | copy-start | bytes 2308
  37.1 36.6 %copy-start.84 = (bf16[384]{0:T(512)(128)(2,1)S(1)}, bf16[384]{0:T(512)(128)(2,1)}, u32[]{:S(2)}) copy-start(bf16[384]{0:T(512)(128)(2,1)} %param.20) | copy-start | bytes 2308
  37.1 40.1 %copy-start.89 = (s32[1,48]{1,0:T(1,128)S(1)}, s32[1,48]{1,0:T(1,128)}, u32[]{:S(2)}) copy-start(s32[1,48]{1,0:T(1,128)} %param.34) | copy-start | bytes 580
  37.1 40.7 %copy-start.85 = (bf16[384]{0:T(512)(128)(2,1)S(1)}, bf16[384]{0:T(512)(128)(2,1)}, u32[]{:S(2)}) copy-start(bf16[384]{0:T(512)(128)(2,1)} %param.27) | copy-start | bytes 2308
  37.1 44.2 %copy-start.86 = (bf16[384]{0:T(512)(128)(2,1)S(1)}, bf16[384]{0:T(512)(128)(2,1)}, u32[]{:S(2)}) copy-start(bf16[384]{0:T(512)(128)(2,1)} %param.26) | copy-start | bytes 2308
  37.2 47.4 %copy-start.87 = (bf16[384]{0:T(512)(128)(2,1)S(1)}, bf16[384]{0:T(512)(128)(2,1)}, u32[]{:S(2)}) copy-start(bf16[384]{0:T(512)(128)(2,1)} %param.32) | copy-start | bytes 2308
  37.2 50.7 %copy-start.88 = (bf16[384]{0:T(512)(128)(2,1)S(1)}, bf16[384]{0:T(512)(128)(2,1)}, u32[]{:S(2)}) copy-start(bf16[384]{0:T(512)(128)(2,1)} %param.33) | copy-start | bytes 2308
  37.2 54.1 %copy-start.57 = (bf16[1,256,768]{2,1,0:T(8,128)(2,1)S(1)}, bf16[1,256,768]{2,1,0:T(8,128)(2,1)}, u32[]{:S(2)}) copy-start(bf16[1,256,768]{2,1,0:T(8,128)(2,1)} %param.18) | copy-start | bytes 1179652
  37.2 174.3 %all-gather.26.cloned.1.call-start = ((), (), s32[]{:S(2)}) async-start(), calls=%async_computation.11 | async-start | bytes 6684672 | tf_op jit(solution)/shard_map/all_gather | solution.py:122
  61.5 179.4 %all-gather.28.cloned.1.call-start = ((), (), s32[]{:S(2)}) async-start(), calls=%async_computation.12 | async-start | bytes 1769472 | tf_op jit(solution)/shard_map/all_gather | solution.py:78
  62.0 236.2 %all-gather.30.cloned.1.call-start = ((), (), s32[]{:S(2)}) async-start(), calls=%async_computation.13 | async-start | bytes 7077888 | tf_op jit(solution)/shard_map/all_gather | solution.py:82
  62.8 299.7 %all-gather.32.cloned.1.call-start = ((), (), s32[]{:S(2)}) async-start(), calls=%async_computation.14 | async-start | bytes 7077888 | tf_op jit(solution)/shard_map/all_gather | solution.py:84
  63.5 590.8 %reduce-scatter.14.cloned.1.call-start = ((), (), s32[]{:S(2)}) async-start(), calls=%async_computation.15 | async-start | bytes 13369344 | tf_op jit(solution)/shard_map/reduce_scatter | solution.py:196
  93.0 58.1 %copy-start.78 = (bf16[256,768]{1,0:T(8,128)(2,1)}, bf16[256,768]{1,0:T(8,128)(2,1)S(1)}, u32[]{:S(2)}) copy-start(bf16[256,768]{1,0:T(8,128)(2,1)S(1)} %fusion.108) | copy-start | bytes 1179652
  173.0 4.3 copy-start.17
  211.5 5.6 copy-start.35
  240.9 57.4 %copy-start.75 = (bf16[256,768]{0,1:T(8,128)(2,1)}, bf16[256,768]{0,1:T(8,128)(2,1)S(1)}, u32[]{:S(2)}) copy-start(bf16[256,768]{0,1:T(8,128)(2,1)S(1)} %fusion.157) | copy-start | bytes 1179652
  310.0 56.5 %copy-start.69 = (bf16[256,3072]{1,0:T(8,128)(2,1)}, bf16[256,3072]{1,0:T(8,128)(2,1)S(1)}, u32[]{:S(2)}) copy-start(bf16[256,3072]{1,0:T(8,128)(2,1)S(1)} %get-tuple-element.124) | copy-start | bytes 4718596
  362.5 6.0 slice-start.6
  362.5 4.3 copy-start.68
  362.5 6.0 slice-start.7
  362.5 6.0 copy-start.91
  367.2 9.4 slice-start.2
  368.3 4.2 slice-start.4
  368.6 8.0 slice-start.3
  377.4 28.2 %copy-start.59 = (bf16[256,768]{1,0:T(8,128)(2,1)}, bf16[256,768]{1,0:T(8,128)(2,1)S(1)}, u32[]{:S(2)}) copy-start(bf16[256,768]{1,0:T(8,128)(2,1)S(1)} %convolution_convert_fusion.18) | copy-start | bytes 1179652
  392.9 4.9 copy-start.13
  400.7 4.9 copy-start.16
  410.0 4.9 copy-start.19
  481.3 6.2 copy-start.39
  481.3 6.2 copy-start.79
  481.3 7.7 copy-start.41
  484.4 5.8 copy-start.43
  487.5 4.2 copy-start.45
  490.3 4.5 copy-start.49
  491.7 4.4 copy-start.51
  493.0 4.5 copy-start.53
  496.1 4.2 copy-start.60
  520.2 158.5 %reduce-scatter.22.cloned.1.call-start = ((), (), s32[]{:S(2)}) async-start(), calls=%async_computation.19 | async-start | bytes 1769472
  521.8 6.2 copy-start.38
  521.8 8.6 copy-start.40
  521.8 16.8 %slice-start = ((s8[6291456]{0:T(1024)(128)(4,1)}), s8[4194304]{0:T(1024)(128)(4,1)S(1)}, s32[]{:S(2)}) async-start(s8[6291456]{0:T(1024)(128)(4,1)} %bitcast.84), calls=%async_computation.22 | async-start | bytes 8388608
  524.0 9.4 copy-start.42
  528.1 7.6 copy-start.44
  530.4 8.2 slice-start.1
  530.4 8.2 copy-start.46
  533.3 6.1 copy-start.48
  535.7 5.1 copy-start.50
  541.6 4.3 copy-start.58
  547.8 155.0 %reduce-scatter.16.cloned.1.call-start = ((), (), s32[]{:S(2)}) async-start(), calls=%async_computation.16 | async-start | bytes 1769472 | tf_op jit(solution)/shard_map/reduce_scatter | solution.py:229
  549.4 216.2 %reduce-scatter.18.cloned.1.call-start = ((), (), s32[]{:S(2)}) async-start(), calls=%async_computation.17 | async-start | bytes 7077888 | tf_op jit(solution)/shard_map/reduce_scatter | solution.py:241
  554.7 274.0 %reduce-scatter.20.cloned.1.call-start = ((), (), s32[]{:S(2)}) async-start(), calls=%async_computation.18 | async-start | bytes 7077888 | tf_op jit(solution)/shard_map/reduce_scatter | solution.py:247
  560.4 292.9 %reduce-scatter.24.cloned.1.call-start = ((), (), s32[]{:S(2)}) async-start(), calls=%async_computation.20 | async-start | bytes 1769472
  655.9 9.7 copy-start.67
  657.4 9.1 copy-start.62
  657.4 220.3 %reduce-scatter.26.cloned.1.call-start = ((), (), s32[]{:S(2)}) async-start(), calls=%async_computation.21 | async-start | bytes 1769472
  659.0 178.1 %copy-start.64 = (bf16[768,768]{1,0:T(8,128)(2,1)S(1)}, bf16[768,768]{1,0:T(8,128)(2,1)}, u32[]{:S(2)}) copy-start(bf16[768,768]{1,0:T(8,128)(2,1)} %all-gather.20.cloned.1.call-done) | copy-start | bytes 3538948
  838.9 40.2 %copy-start.80 = (bf16[384,768]{1,0:T(8,128)(2,1)S(1)}, bf16[384,768]{1,0:T(8,128)(2,1)}, u32[]{:S(2)}) copy-start(bf16[384,768]{1,0:T(8,128)(2,1)} %reduce-scatter.16.cloned.1.call-done) | copy-start | bytes 1769476
  (51 other events, 149.1 us)
Sparse Core Ops, SparseCore 0:
  9.6 24.8 all-gather.19
  36.0 22.7 all-gather.23
  60.4 22.9 all-gather.17
  86.0 62.2 all-gather.21
  151.0 60.4 all-gather.25
  212.9 21.0 all-gather.27
  235.5 62.6 all-gather.29
  299.8 62.6 all-gather.31
  520.4 133.9 reduce-scatter.13
  657.0 21.6 reduce-scatter.21
  681.1 21.7 reduce-scatter.15
  705.6 59.9 reduce-scatter.17
  768.6 59.9 reduce-scatter.19
  831.3 21.8 reduce-scatter.23
  856.0 21.6 reduce-scatter.25
where the time goes:
time: 1200 us
  waiting for transfers between devices  513 us (43%)
  blocking collectives  340 us (28%)
  matrix products  215 us (18%)
  other arithmetic  72.6 us (6%)
  local copies, waits for them, and re-layouts  38.8 us (3%)
  between operations  16.7 us (1%)
    psum x1, blocking collectives, on_device(): totals = lax.psum(tuple(shards), 'ctx')  304 us
    dot_general x30, matrix products, inner_rows(): lax.dot_general(left, right, (((1,), (1,)), ((), ())), preferred_element_...  94.3 us
    reduce_scatter x1, waiting for transfers between devices, on_device(): lax.psum_scatter(key_terms.astype(jnp.bfloat16), 'ctx', scatter_dimension...  94 us
    reduce_scatter x1, waiting for transfers between devices, on_device(): lax.psum_scatter(grad_outer.astype(jnp.bfloat16), 'fsdp', scatter_dimensi...  63 us
    reduce_scatter x1, waiting for transfers between devices, on_device(): lax.psum_scatter(grad_inner.astype(jnp.bfloat16), 'fsdp', scatter_dimensi...  62.8 us
    convert_element_type x12, other arithmetic, on_device(): d_scores = (probs * (d_probs - delta[:, None])).astype(jnp.bfloat16)  56 us
    all_gather x1, waiting for transfers between devices, on_device(): lax.all_gather(key_low, 'ctx', axis=0, tiled=True)  55.3 us
    dot_general x30, matrix products, inner_cols(): lax.dot_general(left, right, (((0,), (0,)), ((), ())), preferred_element_...  54.9 us
  transfers between devices with their start and end apart: 15, of which 13 were waited for; matrix products, arithmetic and copies ran while one was open for 12% of the time, Pallas kernels for 0%

commit v1 on v0

v1 whole, which is shorter than its diff:
```python
import functools
import math

import jax
import jax.numpy as jnp
from jax import lax
from jax.experimental import pallas as pl
from jax.experimental.pallas import tpu as pltpu
from jax.sharding import PartitionSpec as P

H = 12
HD = 64
NG = 4
HG = H // NG
GW = HG * HD

eps = 1e-12
NEG = -1e30
LOG2E = 1.4426950408889634
SCALE = 1.0 / math.sqrt(HD)
bf16 = jnp.bfloat16
f32 = jnp.float32


def layer_norm(r, gain, shift):
    mean = jnp.mean(r, axis=-1, keepdims=True)
    centered = r - mean
    var = jnp.mean(centered * centered, axis=-1, keepdims=True)
    return centered * lax.rsqrt(var + eps) * gain + shift


def gelu_exact(v):
    return jax.nn.gelu(v, approximate=False)


def dot(left, right, ldim=1, rdim=0):
    return lax.dot_general(
        left, right, (((ldim,), (rdim,)), ((), ())), preferred_element_type=f32
    )


def swap(v, axis, bit):
    n = lax.axis_size(axis)
    return lax.ppermute(v, axis, [(i, i ^ bit) for i in range(n)])


def pick(v, index, axis=0):
    return lax.dynamic_index_in_dim(v, index, axis, keepdims=False)


def ordered(bit, own, other):
    return jnp.where(bit == 0, jnp.stack([own, other]), jnp.stack([other, own]))


def slot_of(t, m, g, members):
    shift = members.bit_length() - 1
    return jnp.bitwise_xor(jnp.bitwise_and(t, members - 1), m) * NG + jnp.bitwise_xor(
        jnp.right_shift(t, shift), g
    )


def fwd_kernel(members, block, scal, st_ref, en_ref, q_ref, *rest):
    kv_refs = rest[:members]
    o_ref, ob_ref, lse_ref, k_scr, v_scr = rest[members:]
    m_id, g_id = scal[0], scal[1]
    cols = NG * block
    for s in range(members):
        for h in range(HG):
            k_scr[h, s * cols : (s + 1) * cols, :] = kv_refs[s][h * HD : (h + 1) * HD, :].T
        v_scr[:, s * cols : (s + 1) * cols] = kv_refs[s][GW:, :]
    for j in range(NG):
        qs = slice(j * block, (j + 1) * block)
        start = st_ref[:, qs]
        end = en_ref[:, qs]
        qts = [q_ref[h * HD : (h + 1) * HD, qs] for h in range(HG)]

        def step(t, carry, start=start, end=end, qts=qts):
            off = pl.multiple_of(slot_of(t, m_id, g_id, members) * block, block)
            kpos = t * block + lax.broadcasted_iota(jnp.int32, (block, block), 0)
            allowed = (kpos >= start) & (kpos < end)
            out = []
            for h in range(HG):
                top, total, acc = carry[h]
                s = dot(k_scr[h, pl.ds(off, block), :], qts[h]) * (SCALE * LOG2E)
                s = jnp.where(allowed, s, NEG)
                new = jnp.maximum(top, jnp.max(s, axis=0, keepdims=True))
                alpha = jnp.exp2(top - new)
                p = jnp.exp2(s - new)
                total = total * alpha + jnp.sum(p, axis=0, keepdims=True)
                acc = acc * alpha + dot(
                    v_scr[h * HD : (h + 1) * HD, pl.ds(off, block)], p.astype(bf16)
                )
                out.append((new, total, acc))
            return tuple(out)

        init = tuple(
            (
                jnp.full((1, block), NEG, f32),
                jnp.zeros((1, block), f32),
                jnp.zeros((HD, block), f32),
            )
            for _ in range(HG)
        )
        done = lax.fori_loop(scal[2 + j], scal[2 + NG + j], step, init)
        for h in range(HG):
            top, total, acc = done[h]
            o = acc / total
            o_ref[h * HD : (h + 1) * HD, qs] = o
            ob_ref[h * HD : (h + 1) * HD, qs] = o.astype(bf16)
            lse_ref[h : h + 1, qs] = top + jnp.log2(total)


def bwd_kernel(members, block, scal, st_ref, en_ref, q_ref, o_ref, lse_ref, do_ref, *rest):
    kv_refs = rest[:members]
    dq_ref, dkv_ref, k_scr, v_scr, kt_scr, dk_scr, dv_scr = rest[members:]
    m_id, g_id = scal[0], scal[1]
    cols = NG * block
    for s in range(members):
        part = slice(s * cols, (s + 1) * cols)
        for h in range(HG):
            k_scr[h, part, :] = kv_refs[s][h * HD : (h + 1) * HD, :].T
            v_scr[h, part, :] = kv_refs[s][GW + h * HD : GW + (h + 1) * HD, :].T
        kt_scr[:, part] = kv_refs[s][:GW, :]
    dk_scr[...] = jnp.zeros_like(dk_scr)
    dv_scr[...] = jnp.zeros_like(dv_scr)
    for j in range(NG):
        qs = slice(j * block, (j + 1) * block)
        start = st_ref[:, qs]
        end = en_ref[:, qs]
        per_head = []
        for h in range(HG):
            hr = slice(h * HD, (h + 1) * HD)
            qt = q_ref[hr, qs]
            dot_t = do_ref[hr, qs]
            delta = jnp.sum(dot_t.astype(f32) * o_ref[hr, qs], axis=0, keepdims=True)
            per_head.append((qt, qt.T, dot_t, dot_t.T, delta, lse_ref[h : h + 1, qs]))

        def step(t, carry, start=start, end=end, per_head=per_head):
            off = pl.multiple_of(slot_of(t, m_id, g_id, members) * block, block)
            kpos = t * block + lax.broadcasted_iota(jnp.int32, (block, block), 0)
            allowed = (kpos >= start) & (kpos < end)
            out = []
            for h in range(HG):
                qt, q, dot_t, do, delta, lse = per_head[h]
                s = dot(k_scr[h, pl.ds(off, block), :], qt) * (SCALE * LOG2E)
                p = jnp.where(allowed, jnp.exp2(s - lse), 0.0)
                dp = dot(v_scr[h, pl.ds(off, block), :], dot_t)
                ds = (p * (dp - delta)).astype(bf16)
                dv_scr[h, pl.ds(off, block), :] += dot(p.astype(bf16), do)
                dk_scr[h, pl.ds(off, block), :] += dot(ds, q)
                out.append(
                    carry[h] + dot(kt_scr[h * HD : (h + 1) * HD, pl.ds(off, block)], ds)
                )
            return tuple(out)

        init = tuple(jnp.zeros((HD, block), f32) for _ in range(HG))
        done = lax.fori_loop(scal[2 + j], scal[2 + NG + j], step, init)
        for h in range(HG):
            dq_ref[h * HD : (h + 1) * HD, qs] = (done[h] * SCALE).astype(bf16)
    for s in range(members):
        part = slice(s * cols, (s + 1) * cols)
        for h in range(HG):
            dkv_ref[s, h * HD : (h + 1) * HD, :] = (dk_scr[h, part, :] * SCALE).T.astype(bf16)
            dkv_ref[s, GW + h * HD : GW + (h + 1) * HD, :] = dv_scr[h, part, :].T.astype(bf16)


def whole_specs(n):
    return [pl.BlockSpec(memory_space=pltpu.SMEM)] + [
        pl.BlockSpec(memory_space=pltpu.VMEM) for _ in range(n)
    ]


def attend(members, block, scal, starts, ends, q, kvs):
    keys = members * NG * block
    rows = NG * block
    return pl.pallas_call(
        functools.partial(fwd_kernel, members, block),
        out_shape=(
            jax.ShapeDtypeStruct((GW, rows), f32),
            jax.ShapeDtypeStruct((GW, rows), bf16),
            jax.ShapeDtypeStruct((HG, rows), f32),
        ),
        in_specs=whole_specs(3 + members),
        out_specs=[pl.BlockSpec(memory_space=pltpu.VMEM) for _ in range(3)],
        scratch_shapes=[
            pltpu.VMEM((HG, keys, HD), bf16),
            pltpu.VMEM((GW, keys), bf16),
        ],
        compiler_params=pltpu.CompilerParams(vmem_limit_bytes=50 << 20),
        name="attend",
    )(scal, starts, ends, q, *kvs)


def attend_back(members, block, scal, starts, ends, q, o, lse, do, kvs):
    keys = members * NG * block
    rows = NG * block
    return pl.pallas_call(
        functools.partial(bwd_kernel, members, block),
        out_shape=(
            jax.ShapeDtypeStruct((GW, rows), bf16),
            jax.ShapeDtypeStruct((members, 2 * GW, rows), bf16),
        ),
        in_specs=whole_specs(6 + members),
        out_specs=[pl.BlockSpec(memory_space=pltpu.VMEM) for _ in range(2)],
        scratch_shapes=[
            pltpu.VMEM((HG, keys, HD), bf16),
            pltpu.VMEM((HG, keys, HD), bf16),
            pltpu.VMEM((GW, keys), bf16),
            pltpu.VMEM((HG, keys, HD), f32),
            pltpu.VMEM((HG, keys, HD), f32),
        ],
        compiler_params=pltpu.CompilerParams(vmem_limit_bytes=56 << 20),
        name="attend_back",
    )(scal, starts, ends, q, o, lse, do, *kvs)


def on_device(
    tokens,
    query_weight,
    query_bias,
    key_weight,
    value_weight,
    value_bias,
    out_weight,
    out_bias,
    first_gain,
    first_shift,
    inner_weight,
    inner_bias,
    outer_weight,
    outer_bias,
    second_gain,
    second_shift,
    doc_lengths,
    grad_output,
):
    block = tokens.shape[1]
    width = tokens.shape[2]
    ctx = lax.axis_size("ctx")
    fs = lax.axis_size("fsdp")
    members = ctx // NG
    ci = lax.axis_index("ctx")
    fi = lax.axis_index("fsdp")
    g_id = ci // members
    m_id = ci % members
    core = ci % 2
    own_rows = width // fs
    m_bits = []
    b = members // 2
    while b >= 1:
        m_bits.append(b)
        b //= 2
    g_slots = range(NG)

    def bit_of(index, bit):
        return (index // bit) % 2

    def gather_rows(w):
        rows = w.shape[0]
        if fs != 2:
            return lax.all_gather(w, "fsdp", axis=0, tiled=True)
        half = rows // 2
        mine = swap(lax.dynamic_slice_in_dim(w, core * half, half, 0), "fsdp", 1)
        others = swap(mine, "ctx", 1)
        other = ordered(core, mine, others).reshape(w.shape)
        return ordered(fi, w, other).reshape((2 * rows,) + w.shape[1:])

    local = tokens[0]
    x_slots = {0: local}
    x_slots[2] = swap(local, "ctx", 2 * members)
    x_slots[1] = swap(local, "ctx", members)
    x_slots[3] = swap(x_slots[2], "ctx", members)
    x_all = jnp.concatenate([x_slots[j] for j in g_slots], axis=0)

    vectors = [
        query_bias,
        value_bias,
        out_bias,
        first_gain,
        first_shift,
        inner_bias,
        outer_bias,
        second_gain,
        second_shift,
    ]
    sizes = [v.shape[0] for v in vectors]
    packed = lax.all_gather(jnp.concatenate(vectors), "fsdp", axis=0, tiled=False)
    at = 0
    full = []
    for n in sizes:
        full.append(packed[:, at : at + n].reshape(-1).astype(f32))
        at += n
    qbias, vbias, obias, gain_one, shift_one, ibias, outbias, gain_two, shift_two = full

    group_cols = [
        lax.dynamic_slice_in_dim(w, g_id * GW, GW, 1)
        for w in (query_weight, key_weight, value_weight)
    ]
    w_group = lax.all_gather(
        jnp.concatenate(group_cols, axis=1), "fsdp", axis=0, tiled=True
    ) if fs != 2 else None
    if fs == 2:
        mine = jnp.concatenate(group_cols, axis=1)
        w_group = ordered(fi, mine, swap(mine, "fsdp", 1)).reshape(width, 3 * GW)
    out_full = gather_rows(out_weight)
    inner_full = gather_rows(inner_weight)
    outer_full = gather_rows(outer_weight)
    qkv_full = gather_rows(jnp.concatenate([query_weight, key_weight, value_weight], axis=1))

    bias_group = jnp.concatenate(
        [
            lax.dynamic_slice_in_dim(qbias, g_id * GW, GW, 0),
            jnp.zeros((GW,), f32),
            lax.dynamic_slice_in_dim(vbias, g_id * GW, GW, 0),
        ]
    )
    qkv = (dot(w_group, x_all, 0, 1) + bias_group[:, None]).astype(bf16)
    q_t = qkv[:GW]
    kv_slots = {0: qkv[GW:]}
    for b in m_bits:
        for s in sorted(kv_slots):
            kv_slots[s ^ b] = swap(kv_slots[s], "ctx", b)
    kvs = [kv_slots[s] for s in range(members)]

    doc_ends = jnp.cumsum(doc_lengths[0])
    first = jnp.stack([(jnp.bitwise_xor(g_id, j) * members + m_id) * block for j in g_slots])
    places = (first[:, None] + jnp.arange(block, dtype=jnp.int32)[None, :]).reshape(-1)
    before = places[:, None] >= doc_ends[None, :]
    starts = jnp.max(jnp.where(before, doc_ends[None, :], 0), axis=1).astype(jnp.int32)
    ends = jnp.min(jnp.where(before, ctx * block, doc_ends[None, :]), axis=1).astype(jnp.int32)
    low = starts.reshape(NG, block)[:, 0] // block
    high = (ends.reshape(NG, block)[:, -1] + block - 1) // block
    scal = jnp.concatenate([jnp.stack([m_id, g_id]), low, high]).astype(jnp.int32)
    starts = starts[None]
    ends = ends[None]

    o_t, ob_t, lse = attend(members, block, scal, starts, ends, q_t, kvs)

    def column(v, j):
        return v[:, j * block : (j + 1) * block]

    def exchange(parts):
        return [parts[0]] + [swap(parts[j], "ctx", j * members) for j in range(1, NG)]

    def by_group(slots):
        return [
            lax.select_n(g_id, *[slots[a ^ k] for k in g_slots]) for a in g_slots
        ]

    attn_t = jnp.concatenate(by_group(exchange([column(ob_t, j) for j in g_slots])), axis=0)
    branch = dot(attn_t, out_full, 0, 0) + obias
    local_float = local.astype(f32)
    hidden, first_back = jax.vjp(layer_norm, local_float + branch, gain_one, shift_one)
    hidden_low = hidden.astype(bf16)
    inner = dot(hidden_low, inner_full) + ibias
    active, gelu_back = jax.vjp(gelu_exact, inner)
    active_low = active.astype(bf16)
    outer = dot(active_low, outer_full) + outbias
    result, second_back = jax.vjp(layer_norm, hidden + outer, gain_two, shift_two)
    output = result.astype(bf16)[None]
    grad_y = grad_output[0].astype(f32)
    d_second, grad_gain_two, grad_shift_two = second_back(grad_y)
    d_outer_low = d_second.astype(bf16)
    grad_outbias = jnp.sum(d_outer_low.astype(f32), axis=0)
    (d_inner,) = gelu_back(dot(d_outer_low, outer_full, 1, 1))
    d_inner_low = d_inner.astype(bf16)
    grad_ibias = jnp.sum(d_inner_low.astype(f32), axis=0)
    d_hidden = d_second + dot(d_inner_low, inner_full, 1, 1)
    d_first, grad_gain_one, grad_shift_one = first_back(d_hidden)
    d_branch_low = d_first.astype(bf16)
    grad_obias = jnp.sum(d_branch_low.astype(f32), axis=0)
    do_t = dot(out_full, d_branch_low, 1, 1).astype(bf16).reshape(NG, GW, block)
    do_parts = [pick(do_t, jnp.bitwise_xor(g_id, j)) for j in g_slots]
    do_all = jnp.concatenate(exchange(do_parts), axis=1)

    def halve(acc, axis, bit, index):
        acc = acc.reshape((2, acc.shape[0] // 2) + acc.shape[1:])
        mine = bit_of(index, bit)
        got = swap(pick(acc, 1 - mine), axis, bit)
        return (pick(acc, mine).astype(f32) + got.astype(f32)).astype(bf16)

    def reduce_rows(product, left, bits):
        rows = left.shape[0] // (2 * fs)
        split = left.reshape(fs, 2, rows, left.shape[1])
        send = product(pick(split, 1 - core, 1).reshape(fs * rows, -1)).astype(bf16)
        keep = product(pick(split, core, 1).reshape(fs * rows, -1))
        acc = (keep + swap(send, "ctx", 1).astype(f32)).astype(bf16)
        n = fs
        while n > 1:
            n //= 2
            acc = halve(acc, "fsdp", n, fi)
        for b in bits:
            acc = halve(acc, "ctx", b, ci)
        return acc

    def join(acc, bit):
        both = ordered(bit_of(ci, bit), acc, swap(acc, "ctx", bit))
        return both.reshape((2 * acc.shape[0],) + acc.shape[1:])

    x_bits = [b for b in m_bits if b > 1]
    all_bits = x_bits + [members, 2 * members]

    def weight_grad(left_t, right, rdim=0):
        acc = reduce_rows(lambda part: dot(part, right, 1, rdim), left_t, all_bits)
        for b in all_bits[::-1]:
            acc = join(acc, b)
        return join(acc, 1).astype(f32)

    grad_outer = weight_grad(active_low.T, d_outer_low)
    grad_inner = weight_grad(hidden_low.T, d_inner_low)
    grad_out = weight_grad(attn_t, d_branch_low)

    dq_t, dkv = attend_back(members, block, scal, starts, ends, q_t, o_t, lse, do_all, kvs)
    dkv_slots = {s: dkv[s] for s in range(members)}
    for b in m_bits[::-1]:
        for s in sorted(dkv_slots):
            if s & b:
                got = swap(dkv_slots.pop(s), "ctx", b)
                dkv_slots[s ^ b] = (dkv_slots[s ^ b].astype(f32) + got.astype(f32)).astype(bf16)
    d_qkv = jnp.concatenate([dq_t, dkv_slots[0]], axis=0)
    back = by_group(exchange([column(d_qkv, j) for j in g_slots]))
    d_all = jnp.stack(back).reshape(NG, 3, GW, block).transpose(1, 0, 2, 3).reshape(3 * width, block)
    grad_input = d_first + dot(d_all, qkv_full, 0, 1)

    acc = reduce_rows(lambda part: dot(part, d_qkv, 1, 1), x_all.T, x_bits)
    acc = ordered(bit_of(ci, 2 * members), acc, swap(acc, "ctx", 2 * members))
    acc = ordered(bit_of(ci, members), acc, swap(acc, "ctx", members))
    lead = []
    for b in x_bits[::-1] + [1]:
        acc = ordered(bit_of(ci, b), acc, swap(acc, "ctx", b))
        lead.append(2)
    nb = len(lead)
    acc = acc.astype(f32)
    order = tuple(range(nb)) + (nb + 2, nb + 1, nb, nb + 3)
    acc = acc.transpose(order).reshape(own_rows, NG, 3, GW).transpose(2, 0, 1, 3)
    grad_query, grad_key, grad_value = acc.reshape(3, own_rows, width)

    group_sums = jnp.sum(d_qkv.astype(f32), axis=1)
    spread = (jnp.arange(NG) == g_id)[:, None]
    grad_qbias = jnp.where(spread, group_sums[None, :GW], 0.0).reshape(-1)
    grad_vbias = jnp.where(spread, group_sums[None, 2 * GW :], 0.0).reshape(-1)
    terms = [
        grad_qbias,
        grad_vbias,
        grad_obias,
        grad_gain_one,
        grad_shift_one,
        grad_ibias,
        grad_outbias,
        grad_gain_two,
        grad_shift_two,
    ]
    summed = lax.psum(jnp.concatenate([t.reshape(fs, -1) for t in terms], axis=1), ("fsdp", "ctx"))
    mine = pick(summed, fi)
    shares = []
    at = 0
    for n in sizes:
        shares.append(mine[at : at + n])
        at += n
    s_q, s_v, s_o, s_g1, s_s1, s_i, s_out, s_g2, s_s2 = shares
    return (
        output,
        grad_input[None],
        grad_query,
        s_q,
        grad_key,
        grad_value,
        s_v,
        grad_out,
        s_o,
        s_g1,
        s_s1,
        grad_inner,
        s_i,
        grad_outer,
        s_out,
        s_g2,
        s_s2,
    )


def solution(mesh):
    placed = (
        P("fsdp", "ctx", None),
        P("fsdp", None),
        P("fsdp"),
        P("fsdp", None),
        P("fsdp", None),
        P("fsdp"),
        P("fsdp", None),
        P("fsdp"),
        P("fsdp"),
        P("fsdp"),
        P("fsdp", None),
        P("fsdp"),
        P("fsdp", None),
        P("fsdp"),
        P("fsdp"),
        P("fsdp"),
        P("fsdp", None),
        P("fsdp", "ctx", None),
    )
    return jax.shard_map(
        on_device,
        mesh=mesh,
        in_specs=placed,
        out_specs=(
            P("fsdp", "ctx", None),
            P("fsdp", "ctx", None),
            P("fsdp", None),
            P("fsdp"),
            P("fsdp", None),
            P("fsdp", None),
            P("fsdp"),
            P("fsdp", None),
            P("fsdp"),
            P("fsdp"),
            P("fsdp"),
            P("fsdp", None),
            P("fsdp"),
            P("fsdp", None),
            P("fsdp"),
            P("fsdp"),
            P("fsdp"),
        ),
        check_vma=False,
    )
```

time: 1200 us -> 506 us (0.42)
  waiting for transfers between devices: 513 us -> 90.1 us
  blocking collectives: 340 us -> 71.7 us
  matrix products: 215 us -> 32.8 us
  starting transfers between devices: 0.99 us -> 87.2 us
  Pallas kernels: 0 us -> 71.5 us
  local copies, waits for them, and re-layouts: 38.8 us -> 76.2 us
  between operations: 16.7 us -> 2.26 us
    psum x1, blocking collectives: 304 us -> 45.2 us  [on_device(): lax.psum(jnp.concatenate([t.reshape(fs, -1) for t in terms], axis=1), ('f...]
    reduce_scatter x4 -> x0, waiting for transfers between devices: 242 us -> none  [the longest x1 94 us: on_device(): lax.psum_scatter(key_terms.astype(jnp.bfloat16), 'ctx', scatter_dimension...]
    all_gather x8 -> x0, waiting for transfers between devices: 222 us -> none  [the longest x1 55.3 us: on_device(): lax.all_gather(key_low, 'ctx', axis=0, tiled=True)]
    dot_general x90 -> x16, matrix products: 215 us -> 32.8 us  [dot(): lax.dot_general(left, right, (((ldim,), (rdim,)), ((), ())), preferred_el...]
    ppermute x0 -> x61, waiting for transfers between devices: none -> 90.1 us  [swap(): return lax.ppermute(v, axis, [(i, i ^ bit) for i in range(n)])]
    ppermute x0 -> x61, starting transfers between devices: none -> 87.2 us  [swap(): return lax.ppermute(v, axis, [(i, i ^ bit) for i in range(n)])]
    pallas_call x0 -> x2, Pallas kernels: none -> 71.5 us  [the longest x1 37.1 us: attend_back(): pl.pallas_call(functools.partial(bwd_kernel, members, block), out_shape=(...]
    unnamed x18 -> x0, waiting for transfers between devices: 48.5 us -> none
  transfers between devices with their start and end apart: 15 -> 61, of which waited for: 13 -> 13; matrix products, arithmetic and copies ran while one was open for 12% -> 29% of each run, Pallas kernels for 0% -> 14%
where the time goes in v1:
time: 506 us; the launch traced here: 498 us
  waiting for transfers between devices  90.1 us (18%)
  starting transfers between devices  87.2 us (17%)
  local copies, waits for them, and re-layouts  76.2 us (15%)
  blocking collectives  71.7 us (14%)
  Pallas kernels  71.5 us (14%)
  other arithmetic  65.8 us (13%)
  matrix products  32.8 us (6%)
    ppermute x61, waiting for transfers between devices, swap(): return lax.ppermute(v, axis, [(i, i ^ bit) for i in range(n)])  90.1 us
    ppermute x61, starting transfers between devices, swap(): return lax.ppermute(v, axis, [(i, i ^ bit) for i in range(n)])  87.2 us
    psum x1, blocking collectives, on_device(): lax.psum(jnp.concatenate([t.reshape(fs, -1) for t in terms], axis=1), ('f...  45.2 us
    pallas_call x1, Pallas kernels, attend_back(): pl.pallas_call(functools.partial(bwd_kernel, members, block), out_shape=(...  37.1 us
    pallas_call x1, Pallas kernels, attend(): pl.pallas_call(functools.partial(fwd_kernel, members, block), out_shape=(...  34.4 us
    dot_general x16, matrix products, dot(): lax.dot_general(left, right, (((ldim,), (rdim,)), ((), ())), preferred_el...  32.8 us
    all_gather x1, blocking collectives, on_device(): lax.all_gather(jnp.concatenate(vectors), 'fsdp', axis=0, tiled=False)  26.5 us
    select_n x27, other arithmetic, ordered(): return jnp.where(bit == 0, jnp.stack([own, other]), jnp.stack([other, own]))  25.3 us
  transfers between devices with their start and end apart: 61, of which 13 were waited for; matrix products, arithmetic and copies ran while one was open for 29% of the time, Pallas kernels for 14%

profile of v1, /device:TPU:1, one launch (start us, length us, event | category | flops | bytes accessed | tf_op | source)
XLA Modules:
  0.0 497.5 jit_solution(10205216851516650566)
XLA Ops:
  0.7 3.2 collective-permute-start.2
  18.3 26.5 %all-gather.1 = bf16[2,1,4608]{2,1,0:T(2,128)(2,1)S(1)} all-gather(bf16[1,1,4608]{2,1,0:T(2,128)(2,1)S(1)} %reshape.1106), channel_id=2, replica_groups=mesh['ctx'=16,'fsdp'=2] {'fsdp'}, dimensions={0}, use_global_device_ids=true | all-gather | bytes 27648 | tf_op jit(solution)/shard_map/all_gather | solution.py:287
  44.9 2.4 constant_dynamic-slice_fusion.11
  53.7 2.5 collective-permute-start.11
  58.7 2.6 add_convert_fusion.3
  67.7 2.7 collective-permute-start.4
  70.4 2.5 fusion.55
  72.9 2.6 copy.83
  76.6 5.2 %collective-permute-start.15 = (bf16[768,768]{1,0:T(8,128)(2,1)}, bf16[768,768]{1,0:T(8,128)(2,1)S(1)}, u32[]{:S(2)}, u32[]{:S(2)}) collective-permute-start(bf16[768,768]{1,0:T(8,128)(2,1)} %collective-permute-done.14), channel_id=1, source_target_pairs={{0,2},{2,0},{4,6},{6,4},{8,10},{10,8},{12,14},{14,12},{16,18},{18,... | collective-permute-start | bytes 3538952 | tf_op jit(solution)/shard_map/ppermute | solution.py:44
  81.8 2.9 constant_dynamic-slice_fusion.7
  85.7 16.1 %collective-permute-done.12 = bf16[192,3072]{1,0:T(8,128)(2,1)} collective-permute-done((bf16[192,3072]{1,0:T(8,128)(2,1)}, bf16[192,3072]{1,0:T(8,128)(2,1)}, u32[]{:S(2)}, u32[]{:S(2)}) %collective-permute-start.12) | collective-permute-done | bytes 1179680 | tf_op jit(solution)/shard_map/ppermute | solution.py:44
  101.9 2.8 collective-permute-start.13
  104.8 2.5 maximum_select_fusion.8
  107.3 2.1 maximum_select_fusion.2
  110.3 34.4 %attend.1 = (f32[192,1024]{1,0:T(8,128)S(1)}, bf16[192,1024]{1,0:T(8,128)(2,1)S(1)}, f32[3,1024]{1,0:T(4,128)S(1)}) custom-call(s32[10]{0:T(128)S(1)} %pad_add_fusion.1.scal, s32[1,1024]{1,0:T(1,128)S(1)} %bitcast.345, s32[1,1024]{1,0:T(1,128)S(1)} %bitcast.347, bf16[192,1024]{1,0:T(8,128)(2,1)S(1)} %slice.187.q_ref, bf16[384,1024]{1,0:T(8,128)(2,1)S(1)} %slice.188.rest_0_, ...), custom_call_target="tpu_custom_call" | custom-call | tf_op jit(solution)/shard_map/attend/pallas_call | solution.py:176
  145.1 3.1 collective-permute-start.9
  148.2 2.0 maximum_select_fusion.4
  151.0 2.1 maximum_select_fusion.3
  155.6 7.8 %fusion = (f32[256,3072]{1,0:T(8,128)S(1)}, f32[256,3072]{1,0:T(8,128)S(1)}) fusion(f32[3072]{0:T(1024)S(1)} %reshape.1081, bf16[768,3072]{1,0:T(8,128)(2,1)S(1)} %bitcast.368, f32[256,768]{1,0:T(8,128)S(1)} %get-tuple-element.165, f32[768]{0:T(1024)S(1)} %reshape.1080, f32[768]{0:T(1024)S(1)} %reshape.1079, f32[256]{0:T(256)S(1)} %fusion.63, ...), kind=kOutput, calls=%fused_computation.11 | convolution fusion | flops 1258487808 | bytes 11816960 | tf_op jit(solution)/shard_map/dot_general | solution.py:37
  167.5 2.9 convert_reduce_fusion
  170.4 2.3 multiply_reduce_fusion
  174.8 6.7 %fusion.3 = bf16[3072,256]{0,1:T(8,128)(2,1)S(1)} fusion(f32[256,3072]{1,0:T(8,128)S(1)} %get-tuple-element.167), kind=kLoop, calls=%fused_computation.14 | loop fusion | flops 51118080 | bytes 4718592 | tf_op jit(solution)/shard_map/convert_element_type | solution.py:357
  184.4 2.2 collective-permute-start.17
  187.5 1.9 copy.86
  192.2 3.6 collective-permute-start.36
  199.4 37.1 %attend_back.1 = (bf16[192,1024]{1,0:T(8,128)(2,1)}, bf16[4,384,1024]{2,1,0:T(8,128)(2,1)}) custom-call(s32[10]{0:T(128)} %copy-done.8, s32[1,1024]{1,0:T(1,128)} %bitcast.346, s32[1,1024]{1,0:T(1,128)} %bitcast.348, bf16[192,1024]{1,0:T(8,128)(2,1)} %copy-done.1, f32[192,1024]{1,0:T(8,128)} %copy-done.4, f32[3,1024]{1,0:T(4,128)} %copy-done.7, ...), custom_call_target="tpu_custom_call" | custom-call | tf_op jit(solution)/shard_map/attend_back/pallas_call | solution.py:197
  238.4 2.6 slice_bitcast_fusion.1
  241.7 2.2 convolution_convert_fusion
  250.8 2.7 collective-permute-start.39
  253.5 2.6 fusion.26
  256.1 3.0 collective-permute-start.21
  260.0 4.4 constant_dynamic-slice_fusion.1
  264.3 3.4 copy.94
  268.9 2.3 convolution_convert_fusion.1
  271.1 1.9 collective-permute-start.52
  273.0 2.9 copy.93
  275.9 3.7 collective-permute-done.41
  282.8 2.0 add_convert_fusion.4
  287.8 45.2 %psum.7 = f32[2,4608]{1,0:T(2,128)S(1)} all-reduce(f32[2,4608]{1,0:T(2,128)S(1)} %constant_dynamic-update-slice_fusion.3), channel_id=1, replica_groups=mesh['ctx'=16,'fsdp'=2] {'fsdp','ctx'}, use_global_device_ids=true, to_apply=%region_19.20 | all-reduce | flops 9216 | bytes 73728 | tf_op jit(solution)/shard_map/psum | solution.py:453
  338.0 2.5 add_convert_fusion.1
  341.7 2.0 collective-permute-start.44
  343.7 2.1 select_select_fusion.3
  350.5 25.0 %collective-permute-done.28 = bf16[192,576]{1,0:T(8,128)(2,1)S(1)} collective-permute-done((bf16[192,576]{1,0:T(8,128)(2,1)S(1)}, bf16[192,576]{1,0:T(8,128)(2,1)S(1)}, u32[]{:S(2)}, u32[]{:S(2)}) %collective-permute-start.28) | collective-permute-done | bytes 221216 | tf_op jit(solution)/shard_map/ppermute | solution.py:44
  378.9 2.5 add_convert_fusion
  381.5 2.7 collective-permute-start.30
  388.1 4.2 collective-permute-done.45
  396.3 5.6 %collective-permute-done.46 = bf16[48,3072]{1,0:T(8,128)(2,1)S(1)} collective-permute-done((bf16[48,3072]{1,0:T(8,128)(2,1)S(1)}, bf16[48,3072]{1,0:T(8,128)(2,1)S(1)}, u32[]{:S(2)}, u32[]{:S(2)}) %collective-permute-start.46) | collective-permute-done | bytes 294944 | tf_op jit(solution)/shard_map/ppermute | solution.py:44
  402.2 8.1 %collective-permute-done.53 = bf16[768,768]{1,0:T(8,128)(2,1)S(1)} collective-permute-done((bf16[768,768]{1,0:T(8,128)(2,1)S(1)}, bf16[768,768]{1,0:T(8,128)(2,1)S(1)}, u32[]{:S(2)}, u32[]{:S(2)}) %collective-permute-start.53) | collective-permute-done | bytes 1179680 | tf_op jit(solution)/shard_map/ppermute | solution.py:44
  412.1 11.1 %collective-permute-done.54 = bf16[384,768]{1,0:T(8,128)(2,1)S(1)} collective-permute-done((bf16[384,768]{1,0:T(8,128)(2,1)S(1)}, bf16[384,768]{1,0:T(8,128)(2,1)S(1)}, u32[]{:S(2)}, u32[]{:S(2)}) %collective-permute-start.54) | collective-permute-done | bytes 589856 | tf_op jit(solution)/shard_map/ppermute | solution.py:44
  425.0 4.0 collective-permute-done.55
  429.8 6.8 %collective-permute-done.49 = bf16[48,3072]{1,0:T(8,128)(2,1)S(1)} collective-permute-done((bf16[48,3072]{1,0:T(8,128)(2,1)S(1)}, bf16[48,3072]{1,0:T(8,128)(2,1)S(1)}, u32[]{:S(2)}, u32[]{:S(2)}) %collective-permute-start.49) | collective-permute-done | bytes 294944 | tf_op jit(solution)/shard_map/ppermute | solution.py:44
  439.6 8.6 %collective-permute-start.33 = (bf16[2,2,2,96,576]{4,3,2,1,0:T(8,128)(2,1)S(1)}, bf16[2,2,2,96,576]{4,3,2,1,0:T(8,128)(2,1)S(1)}, u32[]{:S(2)}, u32[]{:S(2)}) collective-permute-start(bf16[2,2,2,96,576]{4,3,2,1,0:T(8,128)(2,1)S(1)} %maximum_select_fusion.14), channel_id=1, source_target_pairs={{0,2},{2,0},{4,6},{6,4},{8,10},{10,8},{12,14},{14,12},{16,18},{18,... | collective-permute-start | bytes 2654216 | tf_op jit(solution)/shard_map/ppermute | solution.py:44
  448.2 2.0 collective-permute-start.58
  451.5 4.1 collective-permute-start.51
  455.6 2.0 fusion.31
  459.8 2.5 convert_bitcast_fusion
  462.3 7.3 %copy.85 = f32[2,2,96,2,2,576]{2,1,0,5,4,3:T(2,128)} copy(f32[2,2,96,2,2,576]{5,2,3,4,1,0:T(8,128)} %convert_bitcast_fusion) | data formatting | bytes 7077888 | tf_op jit(solution)/shard_map/transpose | solution.py:435
  469.6 6.1 %reshape.1104 = f32[384,4,3,192]{0,3,2,1:T(8,128)S(1)} reshape(f32[2,2,96,2,2,576]{2,1,0,5,4,3:T(2,128)} %copy.85) | data formatting | bytes 7077888 | tf_op jit(solution)/shard_map/transpose | solution.py:435
  475.7 1.9 fusion.74
  477.5 2.8 copy.89
  484.9 3.6 collective-permute-start.60
  488.6 2.8 maximum_select_fusion.5
  491.4 2.9 bitcast_convert_fusion.1
  494.7 2.7 bitcast_convert_fusion
  (396 shorter events, 107.7 us)
Async XLA Ops:
  0.7 47.8 %collective-permute-start.2 = (bf16[256,768]{1,0:T(8,128)(2,1)}, bf16[256,768]{1,0:T(8,128)(2,1)}, u32[]{:S(2)}, u32[]{:S(2)}) collective-permute-start(bf16[256,768]{1,0:T(8,128)(2,1)} %bitcast.441), channel_id=1, source_target_pairs={{0,16},{2,18},{4,20},{6,22},{8,24},{10,26},{12,28},{14,30},{16,0},... | collective-permute-start | bytes 1179656 | tf_op jit(solution)/shard_map/ppermute | solution.py:44
  3.9 49.8 %collective-permute-start.1 = (bf16[256,768]{1,0:T(8,128)(2,1)}, bf16[256,768]{1,0:T(8,128)(2,1)}, u32[]{:S(2)}, u32[]{:S(2)}) collective-permute-start(bf16[256,768]{1,0:T(8,128)(2,1)} %bitcast.442), channel_id=1, source_target_pairs={{0,8},{2,10},{4,12},{6,14},{8,0},{10,2},{12,4},{14,6},{16,24},{18,... | collective-permute-start | bytes 1179656 | tf_op jit(solution)/shard_map/ppermute | solution.py:44
  6.9 46.1 %collective-permute-start.10 = (bf16[192,768]{1,0:T(8,128)(2,1)}, bf16[192,768]{1,0:T(8,128)(2,1)}, u32[]{:S(2)}, u32[]{:S(2)}) collective-permute-start(bf16[192,768]{1,0:T(8,128)(2,1)} %constant_dynamic-slice_fusion.12), channel_id=1, source_target_pairs={{0,1},{1,0},{2,3},{3,2},{4,5},{5,4},{6,7},{7,6},{8,9},{9,8},{10,11... | collective-permute-start | bytes 884744 | tf_op jit(solution)/shard_map/ppermute | solution.py:44
  12.5 38.3 %collective-permute-start = (bf16[384,576]{1,0:T(8,128)(2,1)}, bf16[384,576]{1,0:T(8,128)(2,1)}, u32[]{:S(2)}, u32[]{:S(2)}) collective-permute-start(bf16[384,576]{1,0:T(8,128)(2,1)} %pad_maximum_fusion.3), channel_id=1, source_target_pairs={{0,1},{1,0},{2,3},{3,2},{4,5},{5,4},{6,7},{7,6},{8,9},{9,8},{10,11... | collective-permute-start | bytes 1327112 | tf_op jit(solution)/shard_map/ppermute | solution.py:44
  15.0 41.1 %collective-permute-start.25 = (bf16[192,2304]{1,0:T(8,128)(2,1)}, bf16[192,2304]{1,0:T(8,128)(2,1)}, u32[]{:S(2)}, u32[]{:S(2)}) collective-permute-start(bf16[192,2304]{1,0:T(8,128)(2,1)} %constant_dynamic-slice_fusion.9), channel_id=1, source_target_pairs={{0,1},{1,0},{2,3},{3,2},{4,5},{5,4},{6,7},{7,6},{8,9},{9,8},{10,11... | collective-permute-start | bytes 2654216 | tf_op jit(solution)/shard_map/ppermute | solution.py:44
  47.8 61.5 %copy-start.5 = (s32[1024]{0:T(1024)}, s32[1024]{0:T(1024)S(1)}, u32[]{:S(2)}) copy-start(s32[1024]{0:T(1024)S(1)} %get-tuple-element.108) | copy-start | bytes 12292
  47.9 61.5 %copy-start.6 = (s32[1024]{0:T(1024)}, s32[1024]{0:T(1024)S(1)}, u32[]{:S(2)}) copy-start(s32[1024]{0:T(1024)S(1)} %get-tuple-element.109) | copy-start | bytes 12292
  48.5 9.4 %collective-permute-start.3 = (bf16[256,768]{1,0:T(8,128)(2,1)}, bf16[256,768]{1,0:T(8,128)(2,1)S(1)}, u32[]{:S(2)}, u32[]{:S(2)}) collective-permute-start(bf16[256,768]{1,0:T(8,128)(2,1)} %collective-permute-done.2), channel_id=1, source_target_pairs={{0,8},{2,10},{4,12},{6,14},{8,0},{10,2},{12,4},{14,6},{16,24},{18,... | collective-permute-start | bytes 1179656 | tf_op jit(solution)/shard_map/ppermute | solution.py:44
  50.7 25.9 %collective-permute-start.14 = (bf16[768,768]{1,0:T(8,128)(2,1)}, bf16[768,768]{1,0:T(8,128)(2,1)}, u32[]{:S(2)}, u32[]{:S(2)}) collective-permute-start(bf16[768,768]{1,0:T(8,128)(2,1)} %constant_dynamic-slice_fusion.10), channel_id=1, source_target_pairs={{0,1},{1,0},{2,3},{3,2},{4,5},{5,4},{6,7},{7,6},{8,9},{9,8},{10,11... | collective-permute-start | bytes 3538952 | tf_op jit(solution)/shard_map/ppermute | solution.py:44
  53.0 48.8 %collective-permute-start.12 = (bf16[192,3072]{1,0:T(8,128)(2,1)}, bf16[192,3072]{1,0:T(8,128)(2,1)}, u32[]{:S(2)}, u32[]{:S(2)}) collective-permute-start(bf16[192,3072]{1,0:T(8,128)(2,1)} %constant_dynamic-slice_fusion.11), channel_id=1, source_target_pairs={{0,1},{1,0},{2,3},{3,2},{4,5},{5,4},{6,7},{7,6},{8,9},{9,8},{10,11... | collective-permute-start | bytes 3538952 | tf_op jit(solution)/shard_map/ppermute | solution.py:44
  53.7 10.7 %collective-permute-start.11 = (bf16[192,768]{1,0:T(8,128)(2,1)}, bf16[192,768]{1,0:T(8,128)(2,1)S(1)}, u32[]{:S(2)}, u32[]{:S(2)}) collective-permute-start(bf16[192,768]{1,0:T(8,128)(2,1)} %collective-permute-done.10), channel_id=1, source_target_pairs={{0,2},{2,0},{4,6},{6,4},{8,10},{10,8},{12,14},{14,12},{16,18},{18,... | collective-permute-start | bytes 884744 | tf_op jit(solution)/shard_map/ppermute | solution.py:44
  56.2 48.6 %collective-permute-start.26 = (bf16[192,2304]{1,0:T(8,128)(2,1)}, bf16[192,2304]{1,0:T(8,128)(2,1)}, u32[]{:S(2)}, u32[]{:S(2)}) collective-permute-start(bf16[192,2304]{1,0:T(8,128)(2,1)} %collective-permute-done.25), channel_id=1, source_target_pairs={{0,2},{2,0},{4,6},{6,4},{8,10},{10,8},{12,14},{14,12},{16,18},{18,... | collective-permute-start | bytes 2654216 | tf_op jit(solution)/shard_map/ppermute | solution.py:44
  62.3 42.4 %collective-permute-start.5 = (bf16[384,1024]{1,0:T(8,128)(2,1)S(1)}, bf16[384,1024]{1,0:T(8,128)(2,1)S(1)}, u32[]{:S(2)}, u32[]{:S(2)}) collective-permute-start(bf16[384,1024]{1,0:T(8,128)(2,1)S(1)} %slice.188.rest_0_), channel_id=1, source_target_pairs={{0,4},{2,6},{4,0},{6,2},{8,12},{10,14},{12,8},{14,10},{16,20},{18,... | collective-permute-start | bytes 2359304 | tf_op jit(solution)/shard_map/ppermute | solution.py:44
  67.7 41.6 %collective-permute-start.4 = (bf16[384,1024]{1,0:T(8,128)(2,1)S(1)}, bf16[384,1024]{1,0:T(8,128)(2,1)S(1)}, u32[]{:S(2)}, u32[]{:S(2)}) collective-permute-start(bf16[384,1024]{1,0:T(8,128)(2,1)S(1)} %slice.188.rest_0_), channel_id=1, source_target_pairs={{0,2},{2,0},{4,6},{6,4},{8,10},{10,8},{12,14},{14,12},{16,18},{18,... | collective-permute-start | bytes 2359304 | tf_op jit(solution)/shard_map/ppermute | solution.py:44
  76.6 71.6 %collective-permute-start.15 = (bf16[768,768]{1,0:T(8,128)(2,1)}, bf16[768,768]{1,0:T(8,128)(2,1)S(1)}, u32[]{:S(2)}, u32[]{:S(2)}) collective-permute-start(bf16[768,768]{1,0:T(8,128)(2,1)} %collective-permute-done.14), channel_id=1, source_target_pairs={{0,2},{2,0},{4,6},{6,4},{8,10},{10,8},{12,14},{14,12},{16,18},{18,... | collective-permute-start | bytes 3538952 | tf_op jit(solution)/shard_map/ppermute | solution.py:44
  101.9 49.2 %collective-permute-start.13 = (bf16[192,3072]{1,0:T(8,128)(2,1)}, bf16[192,3072]{1,0:T(8,128)(2,1)S(1)}, u32[]{:S(2)}, u32[]{:S(2)}) collective-permute-start(bf16[192,3072]{1,0:T(8,128)(2,1)} %collective-permute-done.12), channel_id=1, source_target_pairs={{0,2},{2,0},{4,6},{6,4},{8,10},{10,8},{12,14},{14,12},{16,18},{18,... | collective-permute-start | bytes 3538952 | tf_op jit(solution)/shard_map/ppermute | solution.py:44
  104.7 4.7 collective-permute-start.6
  144.8 9.4 %collective-permute-start.8 = (bf16[192,256]{1,0:T(8,128)(2,1)S(1)}, bf16[192,256]{1,0:T(8,128)(2,1)S(1)}, u32[]{:S(2)}, u32[]{:S(2)}) collective-permute-start(bf16[192,256]{1,0:T(8,128)(2,1)S(1)} %get-tuple-element.151), channel_id=1, source_target_pairs={{0,16},{2,18},{4,20},{6,22},{8,24},{10,26},{12,28},{14,30},{16,0},... | collective-permute-start | bytes 294920 | tf_op jit(solution)/shard_map/ppermute | solution.py:44
  145.1 9.1 %collective-permute-start.9 = (bf16[192,256]{1,0:T(8,128)(2,1)S(1)}, bf16[192,256]{1,0:T(8,128)(2,1)S(1)}, u32[]{:S(2)}, u32[]{:S(2)}) collective-permute-start(bf16[192,256]{1,0:T(8,128)(2,1)S(1)} %get-tuple-element.152), channel_id=1, source_target_pairs={{0,24},{2,26},{4,28},{6,30},{8,16},{10,18},{12,20},{14,22},{16,8},... | collective-permute-start | bytes 294920 | tf_op jit(solution)/shard_map/ppermute | solution.py:44
  148.2 6.0 %collective-permute-start.7 = (bf16[192,256]{1,0:T(8,128)(2,1)S(1)}, bf16[192,256]{1,0:T(8,128)(2,1)S(1)}, u32[]{:S(2)}, u32[]{:S(2)}) collective-permute-start(bf16[192,256]{1,0:T(8,128)(2,1)S(1)} %get-tuple-element.153), channel_id=1, source_target_pairs={{0,8},{2,10},{4,12},{6,14},{8,0},{10,2},{12,4},{14,6},{16,24},{18,... | collective-permute-start | bytes 294920 | tf_op jit(solution)/shard_map/ppermute | solution.py:44
  170.4 71.3 %copy-start.9 = (bf16[256,3072]{1,0:T(8,128)(2,1)}, bf16[256,3072]{1,0:T(8,128)(2,1)S(1)}, u32[]{:S(2)}) copy-start(bf16[256,3072]{1,0:T(8,128)(2,1)S(1)} %get-tuple-element.113) | copy-start | bytes 4718596
  174.8 6.7 %collective-permute-start.34 = (bf16[384,768]{1,0:T(8,128)(2,1)S(1)}, bf16[384,768]{1,0:T(8,128)(2,1)S(1)}, u32[]{:S(2)}, u32[]{:S(2)}) collective-permute-start(bf16[384,768]{1,0:T(8,128)(2,1)S(1)} %convolution_convert_fusion.2), channel_id=1, source_target_pairs={{0,2},{2,0},{4,6},{6,4},{8,10},{10,8},{12,14},{14,12},{16,18},{18,... | collective-permute-start | bytes 1769480 | tf_op jit(solution)/shard_map/ppermute | solution.py:44
  182.7 8.4 %collective-permute-start.35 = (bf16[192,768]{1,0:T(8,128)(2,1)}, bf16[192,768]{1,0:T(8,128)(2,1)}, u32[]{:S(2)}, u32[]{:S(2)}) collective-permute-start(bf16[192,768]{1,0:T(8,128)(2,1)} %dynamic-slice_bitcast_fusion.6), channel_id=1, source_target_pairs={{0,1},{1,0},{2,3},{3,2},{4,5},{5,4},{6,7},{7,6},{8,9},{9,8},{10,11... | collective-permute-start | bytes 884744 | tf_op jit(solution)/shard_map/ppermute | solution.py:44
  184.0 13.5 %collective-permute-start.18 = (bf16[192,256]{1,0:T(8,128)(2,1)}, bf16[192,256]{1,0:T(8,128)(2,1)}, u32[]{:S(2)}, u32[]{:S(2)}) collective-permute-start(bf16[192,256]{1,0:T(8,128)(2,1)} %get-tuple-element.148), channel_id=1, source_target_pairs={{0,24},{2,26},{4,28},{6,30},{8,16},{10,18},{12,20},{14,22},{16,8},... | collective-permute-start | bytes 294920 | tf_op jit(solution)/shard_map/ppermute | solution.py:44
  184.4 13.1 %collective-permute-start.17 = (bf16[192,256]{1,0:T(8,128)(2,1)}, bf16[192,256]{1,0:T(8,128)(2,1)}, u32[]{:S(2)}, u32[]{:S(2)}) collective-permute-start(bf16[192,256]{1,0:T(8,128)(2,1)} %get-tuple-element.149), channel_id=1, source_target_pairs={{0,16},{2,18},{4,20},{6,22},{8,24},{10,26},{12,28},{14,30},{16,0},... | collective-permute-start | bytes 294920 | tf_op jit(solution)/shard_map/ppermute | solution.py:44
  186.6 10.9 %collective-permute-start.16 = (bf16[192,256]{1,0:T(8,128)(2,1)}, bf16[192,256]{1,0:T(8,128)(2,1)}, u32[]{:S(2)}, u32[]{:S(2)}) collective-permute-start(bf16[192,256]{1,0:T(8,128)(2,1)} %get-tuple-element.150), channel_id=1, source_target_pairs={{0,8},{2,10},{4,12},{6,14},{8,0},{10,2},{12,4},{14,6},{16,24},{18,... | collective-permute-start | bytes 294920 | tf_op jit(solution)/shard_map/ppermute | solution.py:44
  192.2 44.2 %collective-permute-start.36 = (bf16[96,768]{1,0:T(8,128)(2,1)S(1)}, bf16[96,768]{1,0:T(8,128)(2,1)S(1)}, u32[]{:S(2)}, u32[]{:S(2)}) collective-permute-start(bf16[96,768]{1,0:T(8,128)(2,1)S(1)} %dynamic-slice_bitcast_fusion.10), channel_id=1, source_target_pairs={{0,4},{2,6},{4,0},{6,2},{8,12},{10,14},{12,8},{14,10},{16,20},{18,... | collective-permute-start | bytes 442376 | tf_op jit(solution)/shard_map/ppermute | solution.py:44
  236.5 4.5 collective-permute-start.37
  241.0 12.5 %collective-permute-start.20 = (bf16[384,1024]{1,0:T(8,128)(2,1)}, bf16[384,1024]{1,0:T(8,128)(2,1)}, u32[]{:S(2)}, u32[]{:S(2)}) collective-permute-start(bf16[384,1024]{1,0:T(8,128)(2,1)} %get-tuple-element.126), channel_id=1, source_target_pairs={{0,2},{2,0},{4,6},{6,4},{8,10},{10,8},{12,14},{14,12},{16,18},{18,... | collective-permute-start | bytes 2359304 | tf_op jit(solution)/shard_map/ppermute | solution.py:44
  241.7 8.3 %collective-permute-start.38 = (bf16[24,768]{1,0:T(8,128)(2,1)}, bf16[24,768]{1,0:T(8,128)(2,1)}, u32[]{:S(2)}, u32[]{:S(2)}) collective-permute-start(bf16[24,768]{1,0:T(8,128)(2,1)} %dynamic-slice_bitcast_fusion.17), channel_id=1, source_target_pairs={{0,16},{2,18},{4,20},{6,22},{8,24},{10,26},{12,28},{14,30},{16,0},... | collective-permute-start | bytes 110600 | tf_op jit(solution)/shard_map/ppermute | solution.py:44
  248.2 88.3 %collective-permute-start.43 = (bf16[384,3072]{1,0:T(8,128)(2,1)}, bf16[384,3072]{1,0:T(8,128)(2,1)}, u32[]{:S(2)}, u32[]{:S(2)}) collective-permute-start(bf16[384,3072]{1,0:T(8,128)(2,1)} %convolution_convert_fusion), channel_id=1, source_target_pairs={{0,2},{2,0},{4,6},{6,4},{8,10},{10,8},{12,14},{14,12},{16,18},{18,... | collective-permute-start | bytes 7077896 | tf_op jit(solution)/shard_map/ppermute | solution.py:44
  249.9 32.9 %collective-permute-start.19 = (bf16[384,1024]{1,0:T(8,128)(2,1)}, bf16[384,1024]{1,0:T(8,128)(2,1)}, u32[]{:S(2)}, u32[]{:S(2)}) collective-permute-start(bf16[384,1024]{1,0:T(8,128)(2,1)} %get-tuple-element.125), channel_id=1, source_target_pairs={{0,2},{2,0},{4,6},{6,4},{8,10},{10,8},{12,14},{14,12},{16,18},{18,... | collective-permute-start | bytes 2359304 | tf_op jit(solution)/shard_map/ppermute | solution.py:44
  250.8 8.3 %collective-permute-start.39 = (bf16[24,768]{1,0:T(8,128)(2,1)S(1)}, bf16[24,768]{1,0:T(8,128)(2,1)S(1)}, u32[]{:S(2)}, u32[]{:S(2)}) collective-permute-start(bf16[24,768]{1,0:T(8,128)(2,1)S(1)} %fusion.60), channel_id=1, source_target_pairs={{0,16},{2,18},{4,20},{6,22},{8,24},{10,26},{12,28},{14,30},{16,0},... | collective-permute-start | bytes 110600 | tf_op jit(solution)/shard_map/ppermute | solution.py:44
  256.1 26.7 %collective-permute-start.21 = (bf16[384,1024]{1,0:T(8,128)(2,1)}, bf16[384,1024]{1,0:T(8,128)(2,1)}, u32[]{:S(2)}, u32[]{:S(2)}) collective-permute-start(bf16[384,1024]{1,0:T(8,128)(2,1)} %fusion.26), channel_id=1, source_target_pairs={{0,4},{2,6},{4,0},{6,2},{8,12},{10,14},{12,8},{14,10},{16,20},{18,... | collective-permute-start | bytes 2359304 | tf_op jit(solution)/shard_map/ppermute | solution.py:44
  259.7 8.0 %collective-permute-start.40 = (bf16[48,768]{1,0:T(8,128)(2,1)}, bf16[48,768]{1,0:T(8,128)(2,1)}, u32[]{:S(2)}, u32[]{:S(2)}) collective-permute-start(bf16[48,768]{1,0:T(8,128)(2,1)} %bitcast.99), channel_id=1, source_target_pairs={{0,8},{2,10},{4,12},{6,14},{8,0},{10,2},{12,4},{14,6},{16,24},{18,... | collective-permute-start | bytes 221192 | tf_op jit(solution)/shard_map/ppermute | solution.py:44
  268.8 10.8 %collective-permute-start.41 = (bf16[96,768]{1,0:T(8,128)(2,1)S(1)}, bf16[96,768]{1,0:T(8,128)(2,1)S(1)}, u32[]{:S(2)}, u32[]{:S(2)}) collective-permute-start(bf16[96,768]{1,0:T(8,128)(2,1)S(1)} %bitcast.437), channel_id=1, source_target_pairs={{0,4},{2,6},{4,0},{6,2},{8,12},{10,14},{12,8},{14,10},{16,20},{18,... | collective-permute-start | bytes 442376 | tf_op jit(solution)/shard_map/ppermute | solution.py:44
  271.1 107.8 %collective-permute-start.52 = (bf16[1536,768]{1,0:T(8,128)(2,1)}, bf16[1536,768]{1,0:T(8,128)(2,1)}, u32[]{:S(2)}, u32[]{:S(2)}) collective-permute-start(bf16[1536,768]{1,0:T(8,128)(2,1)} %convolution_convert_fusion.1), channel_id=1, source_target_pairs={{0,2},{2,0},{4,6},{6,4},{8,10},{10,8},{12,14},{14,12},{16,18},{18,... | collective-permute-start | bytes 7077896 | tf_op jit(solution)/shard_map/ppermute | solution.py:44
  281.4 53.8 %collective-permute-start.42 = (bf16[192,768]{1,0:T(8,128)(2,1)S(1)}, bf16[192,768]{1,0:T(8,128)(2,1)S(1)}, u32[]{:S(2)}, u32[]{:S(2)}) collective-permute-start(bf16[192,768]{1,0:T(8,128)(2,1)S(1)} %bitcast.415), channel_id=1, source_target_pairs={{0,2},{2,0},{4,6},{6,4},{8,10},{10,8},{12,14},{14,12},{16,18},{18,... | collective-permute-start | bytes 884744 | tf_op jit(solution)/shard_map/ppermute | solution.py:44
  285.8 55.9 %collective-permute-start.24 = (bf16[576,256]{1,0:T(8,128)(2,1)}, bf16[576,256]{1,0:T(8,128)(2,1)}, u32[]{:S(2)}, u32[]{:S(2)}) collective-permute-start(bf16[576,256]{1,0:T(8,128)(2,1)} %get-tuple-element.134), channel_id=1, source_target_pairs={{0,24},{2,26},{4,28},{6,30},{8,16},{10,18},{12,20},{14,22},{16,8},... | collective-permute-start | bytes 884744 | tf_op jit(solution)/shard_map/ppermute | solution.py:44
  286.7 57.0 %collective-permute-start.23 = (bf16[576,256]{1,0:T(8,128)(2,1)}, bf16[576,256]{1,0:T(8,128)(2,1)}, u32[]{:S(2)}, u32[]{:S(2)}) collective-permute-start(bf16[576,256]{1,0:T(8,128)(2,1)} %get-tuple-element.136), channel_id=1, source_target_pairs={{0,16},{2,18},{4,20},{6,22},{8,24},{10,26},{12,28},{14,30},{16,0},... | collective-permute-start | bytes 884744 | tf_op jit(solution)/shard_map/ppermute | solution.py:44
  335.2 8.4 %collective-permute-start.22 = (bf16[576,256]{1,0:T(8,128)(2,1)}, bf16[576,256]{1,0:T(8,128)(2,1)S(1)}, u32[]{:S(2)}, u32[]{:S(2)}) collective-permute-start(bf16[576,256]{1,0:T(8,128)(2,1)} %get-tuple-element.135), channel_id=1, source_target_pairs={{0,8},{2,10},{4,12},{6,14},{8,0},{10,2},{12,4},{14,6},{16,24},{18,... | collective-permute-start | bytes 884744 | tf_op jit(solution)/shard_map/ppermute | solution.py:44
  336.5 9.3 %collective-permute-start.27 = (bf16[384,576]{0,1:T(8,128)(2,1)S(1)}, bf16[384,576]{0,1:T(8,128)(2,1)S(1)}, u32[]{:S(2)}, u32[]{:S(2)}) collective-permute-start(bf16[384,576]{0,1:T(8,128)(2,1)S(1)} %convolution_convert_fusion.3), channel_id=1, source_target_pairs={{0,2},{2,0},{4,6},{6,4},{8,10},{10,8},{12,14},{14,12},{16,18},{18,... | collective-permute-start | bytes 1327112 | tf_op jit(solution)/shard_map/ppermute | solution.py:44
  341.7 35.1 %collective-permute-start.44 = (bf16[192,3072]{1,0:T(8,128)(2,1)}, bf16[192,3072]{1,0:T(8,128)(2,1)}, u32[]{:S(2)}, u32[]{:S(2)}) collective-permute-start(bf16[192,3072]{1,0:T(8,128)(2,1)} %dynamic-slice_bitcast_fusion.1), channel_id=1, source_target_pairs={{0,1},{1,0},{2,3},{3,2},{4,5},{5,4},{6,7},{7,6},{8,9},{9,8},{10,11... | collective-permute-start | bytes 3538952 | tf_op jit(solution)/shard_map/ppermute | solution.py:44
  348.7 26.7 %collective-permute-start.28 = (bf16[192,576]{1,0:T(8,128)(2,1)S(1)}, bf16[192,576]{1,0:T(8,128)(2,1)S(1)}, u32[]{:S(2)}, u32[]{:S(2)}) collective-permute-start(bf16[192,576]{1,0:T(8,128)(2,1)S(1)} %dynamic-slice_bitcast_fusion.7), channel_id=1, source_target_pairs={{0,1},{1,0},{2,3},{3,2},{4,5},{5,4},{6,7},{7,6},{8,9},{9,8},{10,11... | collective-permute-start | bytes 663560 | tf_op jit(solution)/shard_map/ppermute | solution.py:44
  375.6 5.8 %collective-permute-start.29 = (bf16[96,576]{1,0:T(8,128)(2,1)S(1)}, bf16[96,576]{1,0:T(8,128)(2,1)S(1)}, u32[]{:S(2)}, u32[]{:S(2)}) collective-permute-start(bf16[96,576]{1,0:T(8,128)(2,1)S(1)} %dynamic-slice_bitcast_fusion.11), channel_id=1, source_target_pairs={{0,4},{2,6},{4,0},{6,2},{8,12},{10,14},{12,8},{14,10},{16,20},{18,... | collective-permute-start | bytes 331784 | tf_op jit(solution)/shard_map/ppermute | solution.py:44
  378.5 13.8 %collective-permute-start.45 = (bf16[96,3072]{1,0:T(8,128)(2,1)S(1)}, bf16[96,3072]{1,0:T(8,128)(2,1)S(1)}, u32[]{:S(2)}, u32[]{:S(2)}) collective-permute-start(bf16[96,3072]{1,0:T(8,128)(2,1)S(1)} %dynamic-slice_bitcast_fusion.3), channel_id=1, source_target_pairs={{0,4},{2,6},{4,0},{6,2},{8,12},{10,14},{12,8},{14,10},{16,20},{18,... | collective-permute-start | bytes 1769480 | tf_op jit(solution)/shard_map/ppermute | solution.py:44
  381.5 4.9 collective-permute-start.30
  384.2 26.1 %collective-permute-start.53 = (bf16[768,768]{1,0:T(8,128)(2,1)S(1)}, bf16[768,768]{1,0:T(8,128)(2,1)S(1)}, u32[]{:S(2)}, u32[]{:S(2)}) collective-permute-start(bf16[768,768]{1,0:T(8,128)(2,1)S(1)} %dynamic-slice_bitcast_fusion), channel_id=1, source_target_pairs={{0,1},{1,0},{2,3},{3,2},{4,5},{5,4},{6,7},{7,6},{8,9},{9,8},{10,11... | collective-permute-start | bytes 3538952 | tf_op jit(solution)/shard_map/ppermute | solution.py:44
  386.5 8.0 %collective-permute-start.31 = (bf16[2,96,576]{2,1,0:T(8,128)(2,1)S(1)}, bf16[2,96,576]{2,1,0:T(8,128)(2,1)S(1)}, u32[]{:S(2)}, u32[]{:S(2)}) collective-permute-start(bf16[2,96,576]{2,1,0:T(8,128)(2,1)S(1)} %maximum_select_fusion.25), channel_id=1, source_target_pairs={{0,8},{2,10},{4,12},{6,14},{8,0},{10,2},{12,4},{14,6},{16,24},{18,... | collective-permute-start | bytes 663560 | tf_op jit(solution)/shard_map/ppermute | solution.py:44
  392.5 9.4 %collective-permute-start.46 = (bf16[48,3072]{1,0:T(8,128)(2,1)S(1)}, bf16[48,3072]{1,0:T(8,128)(2,1)S(1)}, u32[]{:S(2)}, u32[]{:S(2)}) collective-permute-start(bf16[48,3072]{1,0:T(8,128)(2,1)S(1)} %dynamic-slice_bitcast_fusion.5), channel_id=1, source_target_pairs={{0,8},{2,10},{4,12},{6,14},{8,0},{10,2},{12,4},{14,6},{16,24},{18,... | collective-permute-start | bytes 884744 | tf_op jit(solution)/shard_map/ppermute | solution.py:44
  394.6 44.7 %collective-permute-start.32 = (bf16[2,2,96,576]{3,2,1,0:T(8,128)(2,1)S(1)}, bf16[2,2,96,576]{3,2,1,0:T(8,128)(2,1)S(1)}, u32[]{:S(2)}, u32[]{:S(2)}) collective-permute-start(bf16[2,2,96,576]{3,2,1,0:T(8,128)(2,1)S(1)} %maximum_select_fusion.20), channel_id=1, source_target_pairs={{0,4},{2,6},{4,0},{6,2},{8,12},{10,14},{12,8},{14,10},{16,20},{18,... | collective-permute-start | bytes 1327112 | tf_op jit(solution)/shard_map/ppermute | solution.py:44
  402.0 9.7 %collective-permute-start.47 = (bf16[24,3072]{1,0:T(8,128)(2,1)S(1)}, bf16[24,3072]{1,0:T(8,128)(2,1)S(1)}, u32[]{:S(2)}, u32[]{:S(2)}) collective-permute-start(bf16[24,3072]{1,0:T(8,128)(2,1)S(1)} %dynamic-slice_bitcast_fusion.9), channel_id=1, source_target_pairs={{0,16},{2,18},{4,20},{6,22},{8,24},{10,26},{12,28},{14,30},{16,0},... | collective-permute-start | bytes 442376 | tf_op jit(solution)/shard_map/ppermute | solution.py:44
  410.7 12.5 %collective-permute-start.54 = (bf16[384,768]{1,0:T(8,128)(2,1)S(1)}, bf16[384,768]{1,0:T(8,128)(2,1)S(1)}, u32[]{:S(2)}, u32[]{:S(2)}) collective-permute-start(bf16[384,768]{1,0:T(8,128)(2,1)S(1)} %dynamic-slice_bitcast_fusion.2), channel_id=1, source_target_pairs={{0,4},{2,6},{4,0},{6,2},{8,12},{10,14},{12,8},{14,10},{16,20},{18,... | collective-permute-start | bytes 1769480 | tf_op jit(solution)/shard_map/ppermute | solution.py:44
  411.7 11.7 %collective-permute-start.48 = (bf16[24,3072]{1,0:T(8,128)(2,1)S(1)}, bf16[24,3072]{1,0:T(8,128)(2,1)S(1)}, u32[]{:S(2)}, u32[]{:S(2)}) collective-permute-start(bf16[24,3072]{1,0:T(8,128)(2,1)S(1)} %fusion.53), channel_id=1, source_target_pairs={{0,16},{2,18},{4,20},{6,22},{8,24},{10,26},{12,28},{14,30},{16,0},... | collective-permute-start | bytes 442376 | tf_op jit(solution)/shard_map/ppermute | solution.py:44
  423.4 5.6 %collective-permute-start.55 = (bf16[192,768]{1,0:T(8,128)(2,1)S(1)}, bf16[192,768]{1,0:T(8,128)(2,1)S(1)}, u32[]{:S(2)}, u32[]{:S(2)}) collective-permute-start(bf16[192,768]{1,0:T(8,128)(2,1)S(1)} %dynamic-slice_bitcast_fusion.4), channel_id=1, source_target_pairs={{0,8},{2,10},{4,12},{6,14},{8,0},{10,2},{12,4},{14,6},{16,24},{18,... | collective-permute-start | bytes 884744 | tf_op jit(solution)/shard_map/ppermute | solution.py:44
  423.5 13.1 %collective-permute-start.49 = (bf16[48,3072]{1,0:T(8,128)(2,1)S(1)}, bf16[48,3072]{1,0:T(8,128)(2,1)S(1)}, u32[]{:S(2)}, u32[]{:S(2)}) collective-permute-start(bf16[48,3072]{1,0:T(8,128)(2,1)S(1)} %bitcast.419), channel_id=1, source_target_pairs={{0,8},{2,10},{4,12},{6,14},{8,0},{10,2},{12,4},{14,6},{16,24},{18,... | collective-permute-start | bytes 884744 | tf_op jit(solution)/shard_map/ppermute | solution.py:44
  429.2 8.2 %collective-permute-start.56 = (bf16[96,768]{1,0:T(8,128)(2,1)S(1)}, bf16[96,768]{1,0:T(8,128)(2,1)S(1)}, u32[]{:S(2)}, u32[]{:S(2)}) collective-permute-start(bf16[96,768]{1,0:T(8,128)(2,1)S(1)} %dynamic-slice_bitcast_fusion.8), channel_id=1, source_target_pairs={{0,16},{2,18},{4,20},{6,22},{8,24},{10,26},{12,28},{14,30},{16,0},... | collective-permute-start | bytes 442376 | tf_op jit(solution)/shard_map/ppermute | solution.py:44
  436.7 13.5 %collective-permute-start.50 = (bf16[96,3072]{1,0:T(8,128)(2,1)S(1)}, bf16[96,3072]{1,0:T(8,128)(2,1)S(1)}, u32[]{:S(2)}, u32[]{:S(2)}) collective-permute-start(bf16[96,3072]{1,0:T(8,128)(2,1)S(1)} %bitcast.377), channel_id=1, source_target_pairs={{0,4},{2,6},{4,0},{6,2},{8,12},{10,14},{12,8},{14,10},{16,20},{18,... | collective-permute-start | bytes 1769480 | tf_op jit(solution)/shard_map/ppermute | solution.py:44
  437.4 10.8 %collective-permute-start.57 = (bf16[96,768]{1,0:T(8,128)(2,1)S(1)}, bf16[96,768]{1,0:T(8,128)(2,1)S(1)}, u32[]{:S(2)}, u32[]{:S(2)}) collective-permute-start(bf16[96,768]{1,0:T(8,128)(2,1)S(1)} %fusion.52), channel_id=1, source_target_pairs={{0,16},{2,18},{4,20},{6,22},{8,24},{10,26},{12,28},{14,30},{16,0},... | collective-permute-start | bytes 442376 | tf_op jit(solution)/shard_map/ppermute | solution.py:44
  439.6 20.2 %collective-permute-start.33 = (bf16[2,2,2,96,576]{4,3,2,1,0:T(8,128)(2,1)S(1)}, bf16[2,2,2,96,576]{4,3,2,1,0:T(8,128)(2,1)S(1)}, u32[]{:S(2)}, u32[]{:S(2)}) collective-permute-start(bf16[2,2,2,96,576]{4,3,2,1,0:T(8,128)(2,1)S(1)} %maximum_select_fusion.14), channel_id=1, source_target_pairs={{0,2},{2,0},{4,6},{6,4},{8,10},{10,8},{12,14},{14,12},{16,18},{18,... | collective-permute-start | bytes 2654216 | tf_op jit(solution)/shard_map/ppermute | solution.py:44
  448.2 9.5 %collective-permute-start.58 = (bf16[192,768]{1,0:T(8,128)(2,1)S(1)}, bf16[192,768]{1,0:T(8,128)(2,1)S(1)}, u32[]{:S(2)}, u32[]{:S(2)}) collective-permute-start(bf16[192,768]{1,0:T(8,128)(2,1)S(1)} %bitcast.417), channel_id=1, source_target_pairs={{0,8},{2,10},{4,12},{6,14},{8,0},{10,2},{12,4},{14,6},{16,24},{18,... | collective-permute-start | bytes 884744 | tf_op jit(solution)/shard_map/ppermute | solution.py:44
  451.5 37.1 %collective-permute-start.51 = (bf16[192,3072]{1,0:T(8,128)(2,1)}, bf16[192,3072]{1,0:T(8,128)(2,1)}, u32[]{:S(2)}, u32[]{:S(2)}) collective-permute-start(bf16[192,3072]{1,0:T(8,128)(2,1)} %bitcast.133), channel_id=1, source_target_pairs={{0,2},{2,0},{4,6},{6,4},{8,10},{10,8},{12,14},{14,12},{16,18},{18,... | collective-permute-start | bytes 3538952 | tf_op jit(solution)/shard_map/ppermute | solution.py:44
  458.6 24.5 %collective-permute-start.59 = (bf16[384,768]{1,0:T(8,128)(2,1)}, bf16[384,768]{1,0:T(8,128)(2,1)}, u32[]{:S(2)}, u32[]{:S(2)}) collective-permute-start(bf16[384,768]{1,0:T(8,128)(2,1)} %bitcast.158), channel_id=1, source_target_pairs={{0,4},{2,6},{4,0},{6,2},{8,12},{10,14},{12,8},{14,10},{16,20},{18,... | collective-permute-start | bytes 1769480 | tf_op jit(solution)/shard_map/ppermute | solution.py:44
  484.9 9.3 %collective-permute-start.60 = (bf16[768,768]{1,0:T(8,128)(2,1)S(1)}, bf16[768,768]{1,0:T(8,128)(2,1)S(1)}, u32[]{:S(2)}, u32[]{:S(2)}) collective-permute-start(bf16[768,768]{1,0:T(8,128)(2,1)S(1)} %bitcast.363), channel_id=1, source_target_pairs={{0,2},{2,0},{4,6},{6,4},{8,10},{10,8},{12,14},{14,12},{16,18},{18,... | collective-permute-start | bytes 3538952 | tf_op jit(solution)/shard_map/ppermute | solution.py:44
  (62 other events, 634.9 us)
